TPU v7x, 256 devices: a whole 4x4x8 slice. The times are simulated.
256 devices in a mesh: row: 8 (over y, core), col: 16 (over z, x_hi), wave: 2 (over x_lo).
Axes of the slice: x: 4 (x_hi: 2, x_lo: 2; x = x_hi * 2 + x_lo), y: 4, z: 8, core: 2. Of those that a mesh axis runs over, the one named last changes fastest.
Arguments:
- lower_panel: float32 [16, 64, 4096], P('wave', None, 'col'), may hold values from -1.5 to 1.5
- diag_inverse: float32 [16, 64, 64], P('wave'), may hold values from -0.75 to 0.75
- ancestor_inverse: float32 [16384, 16384], P('row', ('col', 'wave')), may hold values from -0.1875 to 0.1875
- pattern: int32 [16, 32], P('wave'), may hold values from 0 to 127, as said below
Outputs:
- inverse_panel: float32 [16, 64, 16384], P('wave', None, ('row', 'col'))
- diag_block: float32 [16, 64, 64], P('wave')
Inputs may be any that keep to these rules, and one draw needn't show every extreme that they name: `pattern`: each row holds 32 different block numbers in rising order, and every row includes 0, 127 and half of 128.
All inputs are finite; a program needn't handle non-finite values.
Results may differ from a plain program's by a relative error of at most 0.000096.
Values sent between devices are 32-bit elements; how exact they have to be, the bound alone decides.
A program may use at most 128 MiB of HBM per device.

v0:
```python
import jax
import jax.numpy as jnp
from jax import lax
from jax.sharding import Mesh
from jax.sharding import PartitionSpec as P

W = 64
BLK = 128
COL = ("col_0", "col_1")
ROW = ("row_0", "row_1")
ROW_COL = ("row_0", "row_1", "col_0", "col_1")
COL_WAVE = ("col_0", "col_1", "wave")


def swapped(value, axis, distance):
    mask = 2**distance
    pairs = [(source, source ^ mask) for source in range(lax.axis_size(axis))]
    return lax.ppermute(value, axis, pairs)


def sum_by_axis(value, axes, dim):
    for axis in axes:
        value = lax.psum_scatter(value, axis, scatter_dimension=dim, tiled=True)
    return value


def filled_up(lines, peers):
    spare = -len(lines) % peers
    return jnp.pad(lines, [(0, spare)] + [(0, 0)] * (lines.ndim - 1))


def copy_for_each(value, axis):
    copies = jnp.broadcast_to(value, (lax.axis_size(axis), *value.shape))
    return lax.all_to_all(copies, axis, split_axis=0, concat_axis=0, tiled=True)


def joined_along(parts, dim):
    parts = jnp.moveaxis(parts, 0, dim)
    dims = parts.shape
    return parts.reshape(*dims[:dim], dims[dim] * dims[dim + 1], *dims[dim + 2 :])


def gather_axes(value, axes, dim):
    far, near = axes
    parts = copy_for_each(copy_for_each(value, far), near)
    return joined_along(parts.swapaxes(0, 1).reshape(-1, *value.shape), dim)


def split_up(value, dim, peers):
    dims = value.shape
    parts = value.reshape(*dims[:dim], peers, dims[dim] // peers, *dims[dim + 1 :])
    return jnp.moveaxis(parts, dim, 0)


def sum_at_owner(value, axis, dim):
    peers = lax.axis_size(axis)
    parts = lax.all_to_all(split_up(value, dim, peers), axis, 0, 0, tiled=True)
    return jnp.sum(parts, axis=0)


def sum_in_two_steps(value, axes, dim):
    far, near = axes
    parts = split_up(value, dim, lax.axis_size(far))
    nearer = sum_at_owner(parts, near, dim + 1)
    arrived = lax.all_to_all(nearer, far, split_axis=0, concat_axis=0, tiled=True)
    return arrived.sum(axis=0)


def total_of(value, axes):
    lines = value.reshape(-1, value.shape[-1])
    padded = filled_up(lines, lax.axis_size(axes[0]) * lax.axis_size(axes[1]))
    whole = gather_axes(sum_in_two_steps(padded, axes, 0), axes, 0)
    return lax.slice_in_dim(whole, 0, len(lines)).reshape(value.shape)


def select_blocks(pattern, targets):
    return (pattern[:, None, :] == targets[None, :, None]).astype(jnp.float32)


def place_blocks(onehot, packed):
    placed = jnp.einsum("sqk,swkb->swqb", onehot, packed, precision=lax.Precision.HIGHEST)
    return placed.reshape(placed.shape[0] * placed.shape[1], placed.shape[2] * placed.shape[3])


def column_product(left_cols, block_part):
    return lax.dot_general(
        left_cols, block_part, (((1,), (1,)), ((), ())), precision=lax.Precision.HIGHEST
    )


def per_device(lower_panel, diag_inverse, ancestor_inverse, pattern):
    highest = lax.Precision.HIGHEST
    sibs_here = lower_panel.shape[0]
    rows_here, cols_here = ancestor_inverse.shape
    n_col = lax.axis_size(COL)
    n_wave = lax.axis_size("wave")
    row_id = lax.axis_index(ROW)
    col_id = lax.axis_index(COL)
    wave_id = lax.axis_index("wave")
    col_blocks = cols_here // BLK
    rows_blocks = rows_here // BLK
    own_blocks = rows_blocks // n_col
    normed = jnp.einsum("svw,svk->swk", diag_inverse, lower_panel, precision=highest)
    gathered = lax.all_gather(normed, COL, axis=2, tiled=True)
    packed_count = gathered.shape[2] // BLK
    packed = gathered.reshape(sibs_here, W, packed_count, BLK)
    row_targets = (
        row_id * rows_blocks + col_id * own_blocks + jnp.arange(own_blocks, dtype=jnp.int32)
    )
    row_select = select_blocks(pattern, row_targets)
    own_rows = place_blocks(row_select, packed).reshape(sibs_here, W, own_blocks * BLK)
    row_mask = jnp.repeat(jnp.sum(row_select, axis=2), BLK, axis=1)
    partner = swapped(ancestor_inverse, "wave", 0)
    own_targets = (col_id * n_wave + wave_id) * col_blocks + jnp.arange(col_blocks, dtype=jnp.int32)
    other_targets = (col_id * n_wave + (1 - wave_id)) * col_blocks + jnp.arange(
        col_blocks, dtype=jnp.int32
    )
    own_cols = place_blocks(select_blocks(pattern, own_targets), packed)
    other_cols = place_blocks(select_blocks(pattern, other_targets), packed)
    group_sums = -(column_product(own_cols, ancestor_inverse) + column_product(other_cols, partner))
    summed = sum_by_axis(group_sums, COL, 1)
    inverse_panel = summed.reshape(sibs_here, W, own_blocks * BLK) * row_mask[:, None, :]
    update = jnp.einsum("swr,sxr->swx", own_rows, inverse_panel, precision=highest)
    total_update = total_of(update, (("row_0", "row_1", "col_0"), "col_1"))
    base_block = jnp.einsum("svw,svx->swx", diag_inverse, diag_inverse, precision=highest)
    return (inverse_panel, base_block - total_update)


def solution(mesh):
    finer = Mesh(
        mesh.devices.reshape(4, 2, 8, 2, mesh.shape["wave"]),
        ("row_0", "row_1", "col_0", "col_1", "wave"),
    )
    placed = (P("wave", None, COL), P("wave", None, None), P(ROW, COL_WAVE), P("wave", None))
    return jax.shard_map(
        per_device,
        mesh=finer,
        in_specs=placed,
        out_specs=(P("wave", None, ROW_COL), P("wave", None, None)),
        check_vma=False,
    )
```

profile of v0, /device:TPU:1, one launch (start us, length us, event | category | flops | bytes accessed | tf_op | source)
XLA Modules:
  0.0 366.6 jit_solution(3916125529950756266)
XLA Ops:
  7.2 1.0 copy-done
  8.2 2.4 fusion.20
  10.7 2.1 collective-permute-start
  12.8 179.9 %all-gather.2.cloned.1.call-done = f32[8,64,4096]{2,1,0:T(8,128)} async-done(((f32[8,64,256]{2,1,0:T(8,128)}), f32[8,64,4096]{2,1,0:T(8,128)}) %all-gather.2.cloned.1.call-update) | async-done | bytes 8388624 | tf_op jit(solution)/shard_map/all_gather | solution.py:104
  192.7 5.2 %copy.28 = f32[64,8,32,128]{3,2,1,0:T(8,128)S(1)} copy(f32[64,8,32,128]{3,1,2,0:T(8,128)} %bitcast.59) | data formatting | bytes 16777216
  198.0 3.0 fusion.4
  201.0 2.2 copy-done.2
  203.2 7.4 %fusion.8 = f32[512,2048]{1,0:T(8,128)S(1)} fusion(f32[2048,512]{1,0:T(8,128)S(1)} %copy-done.2, f32[64,8,4,128]{3,2,1,0:T(4,128)S(1)} %bitcast.60), kind=kOutput, calls=%fused_computation.10 | convolution fusion | flops 6442450944 | bytes 9437184 | tf_op jit(solution)/shard_map/dot_general | solution.py:86
  210.6 3.0 fusion.2
  213.6 10.2 %add_negate_fusion = f32[512,2048]{1,0:T(8,128)} fusion(f32[512,2048]{1,0:T(8,128)S(1)} %fusion.8, f32[2048,512]{1,0:T(8,128)} %collective-permute-done, f32[64,8,4,128]{3,2,1,0:T(4,128)S(1)} %bitcast.61), kind=kOutput, calls=%fused_computation.6 | convolution fusion | flops 6444548096 | bytes 13631488 | tf_op jit(solution)/shard_map/dot_general | solution.py:86
  223.9 55.6 %reduce-scatter.3.cloned.1.call-done = f32[512,256]{1,0:T(8,128)} async-done(((f32[512,2048]{1,0:T(8,128)}), f32[512,256]{1,0:T(8,128)}) %reduce-scatter.3.cloned.1.call-update) | async-done | bytes 524304 | tf_op jit(solution)/shard_map/reduce_scatter | solution.py:23
  279.5 0.1 convert_reduce_fusion
  279.6 6.5 %fusion = f32[8,1,64,128]{3,1,2,0:T(1,128)S(1)} fusion(pred[8,32,1,1]{1,0,2,3:T(8,128)(4,1)S(1)} %bitcast.68, f32[8,64,32,128]{3,2,1,0:T(8,128)} %bitcast.58), kind=kOutput, calls=%fused_computation | convolution fusion | flops 25165824 | bytes 8651008 | tf_op jit(solution)/shard_map/sqk,swkb->swqb/dot_general | solution.py:81
  286.2 15.6 %reduce-scatter.5.cloned.1.call-done = f32[512,128]{1,0:T(8,128)} async-done(((f32[512,256]{1,0:T(8,128)}), f32[512,128]{1,0:T(8,128)}) %reduce-scatter.5.cloned.1.call-update) | async-done | bytes 262160 | tf_op jit(solution)/shard_map/reduce_scatter | solution.py:23
  301.7 1.0 broadcast_multiply_fusion
  302.8 0.5 fusion.21
  303.4 0.2 reshape.47
  303.6 7.2 %all_to_all.20 = f32[2,1,16384]{2,1,0:T(1,128)S(1)} all-to-all(f32[2,1,16384]{2,1,0:T(1,128)S(1)} %reshape.47), channel_id=1, replica_groups=mesh['row_0'=4,'row_1'=2,'col_0'=8,'col_1'=2,'wave'=2] {'col_1'}, dimensions={0} | all-to-all | bytes 262144 | tf_op jit(solution)/shard_map/all_to_all | solution.py:57
  310.8 0.5 broadcast.16
  311.4 1.0 reduce.2
  312.4 0.2 reshape.48
  312.7 0.1 reshape.49
  312.9 21.3 %all_to_all.21 = f32[64,1,256]{2,1,0:T(1,128)S(1)} all-to-all(f32[64,1,256]{2,1,0:T(1,128)S(1)} %reshape.49), channel_id=1, replica_groups=mesh['row_0'=4,'row_1'=2,'col_0'=8,'col_1'=2,'wave'=2] {'row_0','row_1',..., dimensions={0} | all-to-all | bytes 131072 | tf_op jit(solution)/shard_map/all_to_all | solution.py:65
  334.1 0.8 reduce.3
  335.2 0.1 reshape.51
  335.3 13.7 %all_to_all.22 = f32[64,1,256]{2,1,0:T(1,128)S(1)} all-to-all(f32[64,1,256]{2,1,0:T(1,128)S(1)} %reshape.51), channel_id=1, replica_groups=mesh['row_0'=4,'row_1'=2,'col_0'=8,'col_1'=2,'wave'=2] {'row_0','row_1',..., dimensions={0} | all-to-all | bytes 131072 | tf_op jit(solution)/shard_map/all_to_all | solution.py:34
  349.0 0.8 reduce.4
  350.0 0.2 reshape.53
  350.3 7.2 %all_to_all.23 = f32[2,1,16384]{2,1,0:T(1,128)S(1)} all-to-all(f32[2,1,16384]{2,1,0:T(1,128)S(1)} %reshape.53), channel_id=1, replica_groups=mesh['row_0'=4,'row_1'=2,'col_0'=8,'col_1'=2,'wave'=2] {'col_1'}, dimensions={0} | all-to-all | bytes 262144 | tf_op jit(solution)/shard_map/all_to_all | solution.py:34
  357.5 1.0 reduce.5
  358.5 0.2 reshape.54
  358.8 1.3 convolution_subtract_fusion
  (27 shorter events, 0.8 us)
Async XLA Ops:
  7.2 1.0 copy-start
  7.2 185.5 %all-gather.2.cloned.1.call-start = ((), (), s32[]{:S(2)}) async-start(), calls=%async_computation.6 | async-start | bytes 8912896 | tf_op jit(solution)/shard_map/all_gather | solution.py:104
  10.6 268.8 %reduce-scatter.3.cloned.1.call-start = ((), (), s32[]{:S(2)}) async-start(), calls=%async_computation.7 | async-start | bytes 4718592 | tf_op jit(solution)/shard_map/reduce_scatter | solution.py:23
  10.7 202.9 %collective-permute-start = (f32[2048,512]{1,0:T(8,128)}, f32[2048,512]{1,0:T(8,128)}, u32[]{:S(2)}, u32[]{:S(2)}) collective-permute-start(f32[2048,512]{1,0:T(8,128)} %param.6), channel_id=1, source_target_pairs={{0,1},{1,0},{2,3},{3,2},{4,5},{5,4},{6,7},{7,6},{8,9},{9,8},{10,11... | collective-permute-start | bytes 12582920 | tf_op jit(solution)/shard_map/ppermute | solution.py:18
  192.7 5.2 %copy-start.5 = (s32[8,32]{1,0:T(8,128)S(1)}, s32[8,32]{1,0:T(8,128)}, u32[]{:S(2)}) copy-start(s32[8,32]{1,0:T(8,128)} %param.7) | copy-start | bytes 3076
  198.0 12.7 %copy-start.1 = (f32[64,8,32,128]{3,2,1,0:T(8,128)}, f32[64,8,32,128]{3,2,1,0:T(8,128)S(1)}, u32[]{:S(2)}) copy-start(f32[64,8,32,128]{3,2,1,0:T(8,128)S(1)} %copy.28) | copy-start | bytes 25165828
  198.0 5.2 %copy-start.2 = (f32[2048,512]{1,0:T(8,128)S(1)}, f32[2048,512]{1,0:T(8,128)}, u32[]{:S(2)}) copy-start(f32[2048,512]{1,0:T(8,128)} %param.6) | copy-start | bytes 12582916
  223.8 77.9 %reduce-scatter.5.cloned.1.call-start = ((), (), s32[]{:S(2)}) async-start(), calls=%async_computation.8 | async-start | bytes 786432 | tf_op jit(solution)/shard_map/reduce_scatter | solution.py:23
  286.2 72.6 %copy-start.3 = (f32[8,64,64]{2,1,0:T(8,128)S(1)}, f32[8,64,64]{2,1,0:T(8,128)}, u32[]{:S(2)}) copy-start(f32[8,64,64]{2,1,0:T(8,128)} %param.5) | copy-start | bytes 393220
  302.8 57.3 %copy-start.4 = (f32[8,64,128]{2,1,0:T(8,128)}, f32[8,64,128]{2,1,0:T(8,128)S(1)}, u32[]{:S(2)}) copy-start(f32[8,64,128]{2,1,0:T(8,128)S(1)} %broadcast_multiply_fusion) | copy-start | bytes 786436
Sparse Core Ops, SparseCore 0:
  10.8 181.9 all-gather.1
  224.0 55.4 reduce-scatter.2
  282.0 19.7 reduce-scatter.4
where the time goes:
time: 367 us
  waiting for transfers between devices  251 us (68%)
  blocking collectives  49.4 us (13%)
  matrix products  34.3 us (9%)
  between operations  13.9 us (4%)
  local copies, waits for them, and re-layouts  10.6 us (3%)
  other arithmetic  4.96 us (1%)
    all_gather x1, waiting for transfers between devices, per_device(): gathered = lax.all_gather(normed, COL, axis=2, tiled=True)  180 us
    reduce_scatter x2, waiting for transfers between devices, sum_by_axis(): value = lax.psum_scatter(value, axis, scatter_dimension=dim, tiled=True)  71.2 us
    all_to_all x1, blocking collectives, sum_in_two_steps(): lax.all_to_all(nearer, far, split_axis=0, concat_axis=0, tiled=True)  21.3 us
    all_to_all x2, blocking collectives, copy_for_each(): return lax.all_to_all(copies, axis, split_axis=0, concat_axis=0, tiled=True)  20.9 us
    dot_general x2, matrix products, column_product(): lax.dot_general(left_cols, block_part, (((1,), (1,)), ((), ())), precisio...  17.6 us
    dot_general x3, matrix products, place_blocks(): jnp.einsum('sqk,swkb->swqb', onehot, packed, precision=lax.Precision.HIGH...  12.5 us
    unnamed x21, local copies, waits for them, and re-layouts  9.93 us
  transfers between devices with their start and end apart: 4, of which 3 were waited for; matrix products, arithmetic and copies ran while one was open for 7% of the time, Pallas kernels for 0%

commit v1 on v0

v1 whole, which is shorter than its diff:
```python
import jax
import jax.numpy as jnp
from jax import lax
from jax.experimental import pallas as pl
from jax.experimental.pallas import tpu as pltpu
from jax.sharding import Mesh
from jax.sharding import PartitionSpec as P

W = 64
BLK = 128
Y, CORES, Z, XH, WAVES = 4, 2, 8, 2, 2
ROWS = Y * CORES
COLS = Z * XH
KCOLS = 1024
HALF = KCOLS // 2
COL = ("col_0", "col_1")
ROW = ("row_0", "row_1")
ROW_COL = ("row_0", "row_1", "col_0", "col_1")
COL_WAVE = ("col_0", "col_1", "wave")
MESH = pl.DeviceIdType.MESH
HIGHEST = lax.Precision.HIGHEST
F32 = jnp.float32
BF16 = jnp.bfloat16


def remote(src, dst, send, recv, **device):
    return pltpu.make_async_remote_copy(
        src_ref=src,
        dst_ref=dst,
        send_sem=send,
        recv_sem=recv,
        device_id=device,
        device_id_type=MESH,
    )


def halves(value):
    high = value.astype(BF16)
    return high, (value - high.astype(F32)).astype(BF16)


def dot_last(left, right, precision=None):
    return lax.dot_general(
        left, right, (((1,), (1,)), ((), ())), precision=precision, preferred_element_type=F32
    )


def dot_first(left, right):
    return lax.dot_general(
        left, right, (((0,), (0,)), ((), ())), precision=HIGHEST, preferred_element_type=F32
    )


def kernel(
    table,
    lower,
    diag,
    ancestor,
    panel_out,
    block_out,
    packed,
    dense,
    dense_hi,
    dense_lo,
    abuf,
    a_hi,
    a_lo,
    part,
    ring_in,
    summed,
    cross_in,
    row_blocks,
    own_rows,
    update,
    row_in,
    col_part,
    col_in,
    total,
    a_send,
    a_recv,
    a_loc,
    h_sem,
    zp_send,
    zp_recv,
    zm_send,
    zm_recv,
    w_sem,
    y_send,
    y_recv,
    f_send,
    f_recv,
    c_send,
    c_recv,
    b_send,
    b_recv,
    r_send,
    r_recv,
    x_send,
    x_recv,
    u_send,
    u_recv,
    v_send,
    v_recv,
    t_send,
    t_recv,
):
    y = lax.axis_index("row_0")
    k = lax.axis_index("row_1")
    z = lax.axis_index("col_0")
    h = lax.axis_index("col_1")
    w = lax.axis_index("wave")
    r = y * CORES + k
    c = z * XH + h

    def row_peer(offset):
        other = (r + offset) % ROWS
        return other, {"row_0": other // CORES, "row_1": other % CORES}

    def col_peer(offset):
        other = (c + offset) % COLS
        return other, {"col_0": other // XH, "col_1": other % XH}

    barrier = pltpu.get_barrier_semaphore()

    def greet(device):
        pl.semaphore_signal(barrier, inc=1, device_id=device, device_id_type=MESH)

    greet({"wave": 1 - w})
    greet({"col_1": 1 - h, "wave": 1 - w})
    for offset in range(1, ROWS):
        greet(row_peer(offset)[1])
    for offset in range(1, COLS):
        greet(col_peer(offset)[1])

    local = [
        pltpu.make_async_copy(ancestor.at[d, w], abuf.at[d, w], a_loc.at[d]) for d in range(Z)
    ]
    for copy in local:
        copy.start()
    normed = dot_first(diag[r], lower[r])
    slot = 2 * c
    packed[slot] = normed[:, :BLK]
    packed[slot + 1] = normed[:, BLK:]

    pl.semaphore_wait(barrier, 2 + (ROWS - 1) + (COLS - 1))

    def pair_at(place, side):
        return packed.at[pl.ds(2 * (place * XH + side), 2)]

    trade = remote(pair_at(z, h), pair_at(z, h), h_sem.at[0], h_sem.at[1], col_1=1 - h)
    trade.start()

    a_copies = [
        remote(
            ancestor.at[d, 1 - w], abuf.at[d, w], a_send.at[d], a_recv.at[d], wave=1 - w
        )
        for d in range(Z)
    ]
    z_up, z_down = (z + 1) % Z, (z + Z - 1) % Z

    def z_gather(step, own, up):
        side = h if own == 0 else 1 - h
        source = (z + Z - (step - 1)) % Z if up else (z + step - 1) % Z
        if step < 4:
            view = pair_at(source, side)
        else:
            view = packed.at[pl.ds(2 * (source * XH + side) + (0 if up else 1), 1)]
        send, recv = (zp_send, zp_recv) if up else (zm_send, zm_recv)
        slot_id = 2 * (step - 1) + own
        return remote(
            view, view, send.at[slot_id], recv.at[slot_id], col_0=z_up if up else z_down
        )

    gathers = {}
    for step in range(1, 5):
        for own in range(2):
            if step == 1 and own == 1:
                trade.wait_recv()
            for up in (True, False):
                if step > 1:
                    gathers[step - 1, own, up].wait_recv()
                copy = z_gather(step, own, up)
                copy.start()
                gathers[step, own, up] = copy
        if step <= 3:
            a_copies[step - 1].start()
    for own in range(2):
        for up in (True, False):
            gathers[4, own, up].wait_recv()

    def placed(block):
        found = table[r, block]
        value = packed[jnp.maximum(found - 1, 0)]
        return jnp.where(found > 0, value, jnp.zeros_like(value))

    for j in range(8):
        dense[w, r, :, j * BLK : (j + 1) * BLK] = placed(8 * c + j)

    def spread(group, row, send, recv, **device):
        return remote(dense.at[group, row], dense.at[group, row], send, recv, **device)

    wave_copy = spread(w, r, w_sem.at[0], w_sem.at[1], wave=1 - w)
    wave_copy.start()
    for d in range(3, Z):
        a_copies[d].start()
    y_up, y_down = (y + 1) % Y, (y + Y - 1) % Y
    waves = (w, 1 - w)

    def y_copy(item, up):
        slot_id = 2 * item + (0 if up else 1)
        return spread(
            waves[item], r, y_send.at[slot_id], y_recv.at[slot_id], row_0=y_up if up else y_down
        )

    def core_copy(item, dy):
        row = ((y + dy) % Y) * CORES + k
        slot_id = 4 * item + dy
        return spread(waves[item], row, c_send.at[slot_id], c_recv.at[slot_id], row_1=1 - k)

    y_copies = {(item, up): y_copy(item, up) for item in range(2) for up in (True, False)}
    core_copies = {(item, dy): core_copy(item, dy) for item in range(2) for dy in range(Y)}
    far_up = spread(w, y_down * CORES + k, f_send.at[0], f_recv.at[0], row_0=y_up)
    far_down = spread(1 - w, y_up * CORES + k, f_send.at[1], f_recv.at[1], row_0=y_down)

    y_copies[0, True].start()
    y_copies[0, False].start()
    core_copies[0, 0].start()
    for row in range(ROWS):
        row_blocks[row] = placed(row * COLS + c)
    wave_copy.wait_recv()
    y_copies[1, True].start()
    y_copies[1, False].start()
    core_copies[1, 0].start()
    y_copies[0, True].wait_recv()
    far_up.start()
    core_copies[0, 3].start()
    y_copies[1, False].wait_recv()
    far_down.start()
    core_copies[1, 1].start()
    y_copies[0, False].wait_recv()
    core_copies[0, 1].start()
    y_copies[1, True].wait_recv()
    core_copies[1, 3].start()

    own_rows[r] = row_blocks[r]
    block_copies = []
    for offset in range(1, ROWS):
        other, device = row_peer(offset)
        copy = remote(
            row_blocks.at[other],
            own_rows.at[r],
            b_send.at[offset],
            b_recv.at[offset],
            **device,
        )
        copy.start()
        block_copies.append(copy)

    far_up.wait_recv()
    core_copies[0, 2].start()
    far_down.wait_recv()
    core_copies[1, 2].start()
    for copy in core_copies.values():
        copy.wait_recv()

    def split_dense(index, carry):
        rows = pl.ds(pl.multiple_of(index * W, W), W)
        high, low = halves(dense[index // ROWS, index % ROWS])
        dense_hi[rows, :] = high
        dense_lo[rows, :] = low
        return carry

    lax.fori_loop(0, WAVES * ROWS, split_dense, 0)
    for copy in local:
        copy.wait()
    for copy in a_copies:
        copy.wait_recv()

    def split_ancestor(index, carry):
        for side in range(WAVES):
            high, low = halves(abuf[index, side])
            a_hi[index, :, side * HALF : (side + 1) * HALF] = high
            a_lo[index, :, side * HALF : (side + 1) * HALF] = low
        return carry

    lax.fori_loop(0, Z, split_ancestor, 0)

    def multiply(index, carry):
        first = 2 * (index // 4)
        rows = pl.ds(pl.multiple_of((index % 4) * 256, 256), 256)
        right_hi = a_hi[pl.ds(first, 2)].reshape(2 * BLK, KCOLS)
        right_lo = a_lo[pl.ds(first, 2)].reshape(2 * BLK, KCOLS)
        left_hi, left_lo = dense_hi[rows, :], dense_lo[rows, :]
        product = (
            dot_last(left_hi, right_lo) + dot_last(left_lo, right_hi)
        ) + dot_last(left_hi, right_hi)
        part[first, rows, :] = product[:, :BLK]
        part[first + 1, rows, :] = product[:, BLK:]
        return carry

    lax.fori_loop(0, 16, multiply, 0)

    def ring_place(t, sub):
        return (z + 2 * Z - 1 - t) % Z if sub < 2 else (z + 1 + t) % Z

    def ring_copy(t, sub):
        rows = pl.ds(sub * 256, 256)
        return remote(
            part.at[ring_place(t, sub), rows],
            ring_in.at[t, rows],
            r_send.at[sub, t],
            r_recv.at[sub, t],
            col_0=z_up if sub < 2 else z_down,
        )

    for sub in (0, 2, 1, 3):
        ring_copy(0, sub).start()

    def ring_step(t, carry):
        for sub in (0, 2, 1, 3):
            rows = pl.ds(sub * 256, 256)
            ring_copy(t - 1, sub).wait_recv()
            place = ring_place(t, sub)
            part[place, rows, :] = part[place, rows, :] + ring_in[t - 1, rows, :]
            ring_copy(t, sub).start()
        return carry

    lax.fori_loop(1, Z - 1, ring_step, 0)

    def cross_copy(sub):
        return remote(
            summed.at[pl.ds(sub * 256, 256)],
            cross_in.at[h, pl.ds((sub % 2) * 256, 256)],
            x_send.at[sub],
            x_recv.at[h, sub % 2],
            col_1=w,
            wave=sub // 2,
        )

    def stays(sub):
        return jnp.logical_and(h == w, w == sub // 2)

    for sub in (0, 2, 1, 3):
        rows = pl.ds(sub * 256, 256)
        ring_copy(Z - 2, sub).wait_recv()
        summed[rows, :] = part[z, rows, :] + ring_in[Z - 2, rows, :]

        @pl.when(jnp.logical_not(stays(sub)))
        def _():
            cross_copy(sub).start()

        @pl.when(stays(sub))
        def _():
            cross_in[h, pl.ds((sub % 2) * 256, 256), :] = summed[rows, :]

    for copy in block_copies:
        copy.wait_recv()

    for piece in range(2):
        for side in range(XH):
            rows = pl.ds(piece * 256, 256)

            @pl.when(jnp.logical_not(jnp.logical_and(h == w, h == side)))
            def _():
                remote(
                    summed.at[rows],
                    cross_in.at[side, rows],
                    x_send.at[0],
                    x_recv.at[side, piece],
                    col_1=1 - h,
                ).wait_recv()

    for s in range(ROWS):
        rows = pl.ds(s * W, W)
        value = -(cross_in[0, rows, :] + cross_in[1, rows, :])
        found = table[s, r * COLS + c]
        value = jnp.where(found > 0, value, jnp.zeros_like(value))
        panel_out[s] = value
        lanes = slice((s % 2) * W, (s % 2 + 1) * W)
        update[s // 2, :, lanes] = dot_last(own_rows[s], value, HIGHEST)

    def share(row):
        return update.at[row // CORES, pl.ds((row % CORES) * 32, 32)]

    u_copies = []
    for offset in range(1, ROWS):
        other, device = row_peer(offset)
        copy = remote(
            share(other), row_in.at[offset], u_send.at[offset], u_recv.at[offset], **device
        )
        copy.start()
        u_copies.append(copy)
    partial = update[y, pl.ds(pl.multiple_of(k * 32, 32), 32), :]
    for offset in range(1, ROWS):
        u_copies[offset - 1].wait_recv()
        partial = partial + row_in[offset]
    col_part[...] = partial
    v_copies = []
    for offset in range(1, COLS):
        copy = remote(
            col_part, col_in.at[offset], v_send.at[offset], v_recv.at[offset], **col_peer(offset)[1]
        )
        copy.start()
        v_copies.append(copy)
    col_in[0] = col_part[...]
    for copy in v_copies:
        copy.wait_recv()
    whole = col_in[c]
    for owner in range(1, COLS):
        whole = whole + col_in[(c + COLS - owner) % COLS]
    mine = pl.ds(pl.multiple_of(k * 32, 32), 32)
    total[y, mine, :] = whole
    t_copies = []
    for offset in range(1, ROWS):
        copy = remote(
            total.at[y, mine],
            total.at[y, mine],
            t_send.at[offset],
            t_recv.at[offset],
            **row_peer(offset)[1],
        )
        copy.start()
        t_copies.append(copy)
    for copy in t_copies:
        copy.wait_recv()
    for s in range(ROWS):
        base = dot_first(diag[s], diag[s])
        lanes = slice((s % 2) * W, (s % 2 + 1) * W)
        block_out[s] = base - total[s // 2, :, lanes]

    trade.wait_send()
    for copy in gathers.values():
        copy.wait_send()
    for copy in a_copies:
        copy.wait_send()
    wave_copy.wait_send()
    for copy in y_copies.values():
        copy.wait_send()
    for copy in core_copies.values():
        copy.wait_send()
    far_up.wait_send()
    far_down.wait_send()
    for copy in block_copies + u_copies + v_copies + t_copies:
        copy.wait_send()

    def ring_sent(t, carry):
        for sub in range(4):
            ring_copy(t, sub).wait_send()
        return carry

    lax.fori_loop(0, Z - 1, ring_sent, 0)
    for sub in range(4):

        @pl.when(jnp.logical_not(stays(sub)))
        def _():
            cross_copy(sub).wait_send()


def per_device(lower_panel, diag_inverse, ancestor_inverse, pattern):
    blocks = jnp.arange(R_BLOCKS, dtype=jnp.int32)
    places = jnp.arange(1, pattern.shape[1] + 1, dtype=jnp.int32)
    hits = pattern[:, None, :] == blocks[None, :, None]
    table = jnp.max(jnp.where(hits, places[None, None, :], 0), axis=2)
    ancestor = ancestor_inverse.reshape(Z, XH, BLK, HALF)
    vmem = pl.BlockSpec(memory_space=pltpu.VMEM)
    dma = pltpu.SemaphoreType.DMA
    return pl.pallas_call(
        kernel,
        out_shape=(
            jax.ShapeDtypeStruct((ROWS, W, BLK), F32),
            jax.ShapeDtypeStruct((ROWS, W, W), F32),
        ),
        in_specs=[
            pl.BlockSpec(memory_space=pltpu.SMEM),
            vmem,
            vmem,
            pl.BlockSpec(memory_space=pl.ANY),
        ],
        out_specs=(vmem, vmem),
        scratch_shapes=[
            pltpu.VMEM((32, W, BLK), F32),
            pltpu.VMEM((WAVES, ROWS, W, KCOLS), F32),
            pltpu.VMEM((WAVES * ROWS * W, KCOLS), BF16),
            pltpu.VMEM((WAVES * ROWS * W, KCOLS), BF16),
            pltpu.VMEM((Z, WAVES, BLK, HALF), F32),
            pltpu.VMEM((Z, BLK, KCOLS), BF16),
            pltpu.VMEM((Z, BLK, KCOLS), BF16),
            pltpu.VMEM((Z, WAVES * ROWS * W, BLK), F32),
            pltpu.VMEM((Z - 1, WAVES * ROWS * W, BLK), F32),
            pltpu.VMEM((WAVES * ROWS * W, BLK), F32),
            pltpu.VMEM((XH, ROWS * W, BLK), F32),
            pltpu.VMEM((ROWS, W, BLK), F32),
            pltpu.VMEM((ROWS, W, BLK), F32),
            pltpu.VMEM((Y, W, BLK), F32),
            pltpu.VMEM((ROWS, 32, BLK), F32),
            pltpu.VMEM((32, BLK), F32),
            pltpu.VMEM((COLS, 32, BLK), F32),
            pltpu.VMEM((Y, W, BLK), F32),
            dma((Z,)),
            dma((Z,)),
            dma((Z,)),
            dma((2,)),
            dma((8,)),
            dma((8,)),
            dma((8,)),
            dma((8,)),
            dma((2,)),
            dma((4,)),
            dma((4,)),
            dma((2,)),
            dma((2,)),
            dma((8,)),
            dma((8,)),
            dma((ROWS,)),
            dma((ROWS,)),
            dma((4, Z - 1)),
            dma((4, Z - 1)),
            dma((4,)),
            dma((2, 2)),
            dma((ROWS,)),
            dma((ROWS,)),
            dma((COLS,)),
            dma((COLS,)),
            dma((ROWS,)),
            dma((ROWS,)),
        ],
        compiler_params=pltpu.CompilerParams(
            collective_id=0, has_side_effects=True, vmem_limit_bytes=60 * 1024 * 1024
        ),
        name="wave",
    )(table, lower_panel, diag_inverse, ancestor)


R_BLOCKS = 128


def solution(mesh):
    finer = Mesh(
        mesh.devices.reshape(Y, CORES, Z, XH, WAVES),
        ("row_0", "row_1", "col_0", "col_1", "wave"),
    )
    placed = (P("wave", None, COL), P("wave", None, None), P(ROW, COL_WAVE), P("wave", None))
    return jax.shard_map(
        per_device,
        mesh=finer,
        in_specs=placed,
        out_specs=(P("wave", None, ROW_COL), P("wave", None, None)),
        check_vma=False,
    )
```

time: 367 us -> 151 us (0.41)
  waiting for transfers between devices: 251 us -> 0 us
  Pallas kernels: 0 us -> 145 us
  blocking collectives: 49.4 us -> 0 us
  matrix products: 34.3 us -> 0 us
  between operations: 13.9 us -> 0.64 us
  local copies, waits for them, and re-layouts: 10.6 us -> 3.34 us
    all_gather x1 -> x0, waiting for transfers between devices: 180 us -> none  [per_device(): gathered = lax.all_gather(normed, COL, axis=2, tiled=True)]
    pallas_call x0 -> x1, Pallas kernels: none -> 145 us  [per_device(): pl.pallas_call(kernel, out_shape=(jax.ShapeDtypeStruct((ROWS, W, BLK), F3...]
    reduce_scatter x2 -> x0, waiting for transfers between devices: 71.2 us -> none  [sum_by_axis(): value = lax.psum_scatter(value, axis, scatter_dimension=dim, tiled=True)]
    all_to_all x4 -> x0, blocking collectives: 49.4 us -> none  [the longest x1 21.3 us: sum_in_two_steps(): lax.all_to_all(nearer, far, split_axis=0, concat_axis=0, tiled=True)]
    dot_general x8 -> x0, matrix products: 34.3 us -> none  [the longest x2 17.6 us: column_product(): lax.dot_general(left_cols, block_part, (((1,), (1,)), ((), ())), precisio...]
    unnamed x21 -> x2, local copies, waits for them, and re-layouts: 9.93 us -> 3.34 us
  transfers between devices with their start and end apart: 4 -> 0, of which waited for: 3 -> 0; matrix products, arithmetic and copies ran while one was open for 7% -> 0% of each run, Pallas kernels for 0% -> 0%
where the time goes in v1:
time: 151 us
  Pallas kernels  145 us (96%)
  local copies, waits for them, and re-layouts  3.34 us (2%)
    pallas_call x1, Pallas kernels, per_device(): pl.pallas_call(kernel, out_shape=(jax.ShapeDtypeStruct((ROWS, W, BLK), F3...  145 us
    unnamed x2, local copies, waits for them, and re-layouts  3.34 us

profile of v1, /device:TPU:1, one launch (start us, length us, event | category | flops | bytes accessed | tf_op | source)
XLA Modules:
  0.0 150.5 jit_solution(4819420142429875215)
XLA Ops:
  0.6 1.4 select_reduce_fusion.table
  2.0 145.1 %wave.1 = (f32[8,64,128]{2,1,0:T(8,128)}, f32[8,64,64]{2,1,0:T(8,128)}) custom-call(s32[8,128]{1,0:T(8,128)} %select_reduce_fusion.table, f32[8,64,256]{2,1,0:T(8,128)} %lower.1, f32[8,64,64]{2,1,0:T(8,128)} %diag.1, f32[8,2,128,512]{3,2,1,0:T(8,128)} %bitcast.1), custom_call_target="tpu_custom_call" | custom-call | tf_op jit(solution)/shard_map/wave/pallas_call | solution.py:467
  147.2 1.7 %copy.8 = f32[8,64,128]{2,1,0:T(8,128)} copy(f32[8,64,128]{2,1,0:T(8,128)} %get-tuple-element.4) | data formatting | bytes 524288
  148.8 1.7 %copy.9 = f32[8,64,64]{2,1,0:T(8,128)} copy(f32[8,64,64]{2,1,0:T(8,128)} %get-tuple-element.5) | data formatting | bytes 262144
  (1 shorter events, 0.0 us)

commit v2 on v1

v2 whole, which is shorter than its diff:
```python
import jax
import jax.numpy as jnp
from jax import lax
from jax.experimental import pallas as pl
from jax.experimental.pallas import tpu as pltpu
from jax.sharding import Mesh
from jax.sharding import PartitionSpec as P

W = 64
BLK = 128
Y, CORES, Z, XH, WAVES = 4, 2, 8, 2, 2
ROWS = Y * CORES
COLS = Z * XH
KCOLS = 1024
HALF = KCOLS // 2
COL = ("col_0", "col_1")
ROW = ("row_0", "row_1")
ROW_COL = ("row_0", "row_1", "col_0", "col_1")
COL_WAVE = ("col_0", "col_1", "wave")
MESH = pl.DeviceIdType.MESH
HIGHEST = lax.Precision.HIGHEST
F32 = jnp.float32
BF16 = jnp.bfloat16


def remote(src, dst, send, recv, **device):
    return pltpu.make_async_remote_copy(
        src_ref=src,
        dst_ref=dst,
        send_sem=send,
        recv_sem=recv,
        device_id=device,
        device_id_type=MESH,
    )


def halves(value):
    high = value.astype(BF16)
    return high, (value - high.astype(F32)).astype(BF16)


def dot_last(left, right, precision=None):
    return lax.dot_general(
        left, right, (((1,), (1,)), ((), ())), precision=precision, preferred_element_type=F32
    )


def dot_first(left, right):
    return lax.dot_general(
        left, right, (((0,), (0,)), ((), ())), precision=HIGHEST, preferred_element_type=F32
    )


def kernel(
    pattern,
    lower_hbm,
    diag_hbm,
    ancestor,
    panel_out,
    block_out,
    lower,
    diag,
    packed,
    dense,
    dense_hi,
    dense_lo,
    abuf,
    a_hi,
    a_lo,
    part,
    up_in,
    down_in,
    summed,
    cross_in,
    row_blocks,
    own_rows,
    update,
    row_in,
    col_in,
    total,
    held,
    in_sem,
    a_send,
    a_recv,
    a_loc,
    h_sem,
    zp_send,
    zp_recv,
    zm_send,
    zm_recv,
    w_sem,
    y_send,
    y_recv,
    f_send,
    f_recv,
    c_send,
    c_recv,
    b_send,
    b_recv,
    up_send,
    up_recv,
    down_send,
    down_recv,
    x_send,
    x_recv,
    u_send,
    u_recv,
    v_send,
    v_recv,
    t_send,
    t_recv,
):
    y = lax.axis_index("row_0")
    k = lax.axis_index("row_1")
    z = lax.axis_index("col_0")
    h = lax.axis_index("col_1")
    w = lax.axis_index("wave")
    r = y * CORES + k
    c = z * XH + h

    def row_peer(offset):
        other = (r + offset) % ROWS
        return other, {"row_0": other // CORES, "row_1": other % CORES}

    def side_peer(offset):
        other, device = row_peer(offset // XH)
        side = (h + offset % XH) % XH
        return other, side, {**device, "col_1": side}

    barrier = pltpu.get_barrier_semaphore()

    def greet(device):
        pl.semaphore_signal(barrier, inc=1, device_id=device, device_id_type=MESH)

    take_lower = pltpu.make_async_copy(lower_hbm.at[r], lower, in_sem.at[0])
    take_diag = pltpu.make_async_copy(diag_hbm, diag, in_sem.at[1])
    take_lower.start()
    take_diag.start()
    for offset in range(1, Z):
        greet({"col_0": (z + offset) % Z})
    for offset in range(1, ROWS * XH):
        greet(side_peer(offset)[2])
    greet({"wave": 1 - w})
    greet({"col_1": 1 - h, "wave": 1 - w})

    places = [(z + offset) % Z for offset in (4, 3, 5, 2, 6, 1, 7, 0)]
    local = [
        pltpu.make_async_copy(ancestor.at[places[d], w], abuf.at[d, w], a_loc.at[d])
        for d in range(Z)
    ]
    for copy in local:
        copy.start()
    take_lower.wait()
    take_diag.wait()
    normed = dot_first(diag[r], lower[...])
    slot = 2 * c
    packed[slot] = normed[:, :BLK]
    packed[slot + 1] = normed[:, BLK:]

    own_block = r * COLS + c
    wanted = [8 * c + j for j in range(8)] + [row * COLS + c for row in range(ROWS)]

    def look(m, carry):
        block = pattern[r, m]
        found = [jnp.where(block == goal, m + 1, old) for goal, old in zip(wanted, carry[:16])]
        kept = [
            jnp.where(pattern[s, m] == own_block, 1, old) for s, old in enumerate(carry[16:])
        ]
        return tuple(found + kept)

    looked = lax.fori_loop(0, 32, look, (jnp.int32(0),) * 24)
    for s in range(ROWS):
        held[s] = looked[16 + s]

    pl.semaphore_wait(barrier, 2 + (ROWS * XH - 1) + (Z - 1))

    def pair_at(place, side):
        return packed.at[pl.ds(2 * (place * XH + side), 2)]

    trade = remote(pair_at(z, h), pair_at(z, h), h_sem.at[0], h_sem.at[1], col_1=1 - h)
    trade.start()

    a_copies = [
        remote(
            ancestor.at[places[d], 1 - w],
            abuf.at[d, w],
            a_send.at[d],
            a_recv.at[d],
            wave=1 - w,
        )
        for d in range(Z)
    ]
    z_up, z_down = (z + 1) % Z, (z + Z - 1) % Z

    def z_gather(step, own, up):
        side = h if own == 0 else 1 - h
        source = (z + Z - (step - 1)) % Z if up else (z + step - 1) % Z
        if step < 4:
            view = pair_at(source, side)
        else:
            view = packed.at[pl.ds(2 * (source * XH + side) + (0 if up else 1), 1)]
        send, recv = (zp_send, zp_recv) if up else (zm_send, zm_recv)
        slot_id = 2 * (step - 1) + own
        return remote(
            view, view, send.at[slot_id], recv.at[slot_id], col_0=z_up if up else z_down
        )

    gathers = {}
    for step in range(1, 5):
        for own in range(2):
            if step == 1 and own == 1:
                trade.wait_recv()
            for up in (True, False):
                if step > 1:
                    gathers[step - 1, own, up].wait_recv()
                copy = z_gather(step, own, up)
                copy.start()
                gathers[step, own, up] = copy
        if step <= 2:
            a_copies[step - 1].start()
    for s in range(ROWS):
        block_out[s] = dot_first(diag[s], diag[s])
    for own in range(2):
        for up in (True, False):
            gathers[4, own, up].wait_recv()

    def placed(found):
        value = packed[jnp.maximum(found - 1, 0)]
        return jnp.where(found > 0, value, jnp.zeros_like(value))

    for j in range(8):
        dense[0, :, j * BLK : (j + 1) * BLK] = placed(looked[j])

    def spot(item, dy, core):
        return (item * Y + dy) * CORES + core

    def spread(source, target, send, recv, **device):
        return remote(
            dense.at[spot(*source)], dense.at[spot(*target)], send, recv, **device
        )

    y_up, y_down = (y + 1) % Y, (y + Y - 1) % Y
    waves = (w, 1 - w)

    def y_copy(item, up):
        slot_id = 2 * item + (0 if up else 1)
        return spread(
            (item, 0, 0),
            (item, 3 if up else 1, 0),
            y_send.at[slot_id],
            y_recv.at[slot_id],
            row_0=y_up if up else y_down,
        )

    def core_copy(item, dy):
        slot_id = 4 * item + dy
        return spread(
            (item, dy, 0), (item, dy, 1), c_send.at[slot_id], c_recv.at[slot_id], row_1=1 - k
        )

    wave_copy = spread((0, 0, 0), (1, 0, 0), w_sem.at[0], w_sem.at[1], wave=1 - w)
    y_copies = {(item, up): y_copy(item, up) for item in range(2) for up in (True, False)}
    core_copies = {(item, dy): core_copy(item, dy) for item in range(2) for dy in range(Y)}
    far_up = spread((0, 3, 0), (0, 2, 0), f_send.at[0], f_recv.at[0], row_0=y_up)
    far_down = spread((1, 1, 0), (1, 2, 0), f_send.at[1], f_recv.at[1], row_0=y_down)

    units = ((0, 0), (0, 1), (0, 3), (1, 0), (0, 2), (1, 1), (1, 3), (1, 2))

    def split_unit(unit):
        item, dy = units[unit]
        core_copies[item, dy].wait_recv()
        for core in range(CORES):
            rows = slice(unit * BLK + core * W, unit * BLK + (core + 1) * W)
            high, low = halves(dense[spot(item, dy, core)])
            dense_hi[rows, :] = high
            dense_lo[rows, :] = low

    def split_ancestor(d):
        local[d].wait()
        a_copies[d].wait_recv()
        for side in range(WAVES):
            high, low = halves(abuf[d, side])
            a_hi[d, :, side * HALF : (side + 1) * HALF] = high
            a_lo[d, :, side * HALF : (side + 1) * HALF] = low

    def multiply(group, first, count):
        right_hi = a_hi[first : first + count].reshape(count * BLK, KCOLS)
        right_lo = a_lo[first : first + count].reshape(count * BLK, KCOLS)
        for start in range(group * 512, group * 512 + 512, 256):
            rows = slice(start, start + 256)
            left_hi, left_lo = dense_hi[rows, :], dense_lo[rows, :]
            product = (
                dot_last(left_hi, right_lo) + dot_last(left_lo, right_hi)
            ) + dot_last(left_hi, right_hi)
            for d in range(count):
                part[first + d, rows, :] = product[:, d * BLK : (d + 1) * BLK]

    def rows_of(unit):
        return pl.ds(unit * BLK, BLK)

    def chain(t, unit, up):
        slot_id = 0 if t == 0 else (2 * t - 1 if up else 2 * t)
        send, recv, into = (up_send, up_recv, up_in) if up else (down_send, down_recv, down_in)
        return remote(
            part.at[slot_id, rows_of(unit)],
            into.at[t, rows_of(unit)],
            send.at[t, unit],
            recv.at[t, unit],
            col_0=z_up if up else z_down,
        )

    chains = []

    def send_on(t, unit, up):
        copy = chain(t, unit, up)
        copy.start()
        chains.append(copy)

    def first_step(group):
        for unit in range(4 * group, 4 * group + 4):
            send_on(0, unit, unit % 2 == 0)

    def next_step(group, t):
        for unit in range(4 * group, 4 * group + 4):
            for up in (True, False):
                if t > 1 or (unit % 2 == 0) == up:
                    chain(t - 1, unit, up).wait_recv()
                    slot_id = 2 * t - 1 if up else 2 * t
                    into = up_in if up else down_in
                    part[slot_id, rows_of(unit), :] = (
                        part[slot_id, rows_of(unit), :] + into[t - 1, rows_of(unit), :]
                    )
                send_on(t, unit, up)

    def cross_copy(unit):
        item, dy = units[unit]
        return remote(
            summed.at[rows_of(unit)],
            cross_in.at[h, dy],
            x_send.at[unit],
            x_recv.at[h, dy],
            col_1=w,
            wave=waves[item],
        )

    def last_step(group):
        for unit in range(4 * group, 4 * group + 4):
            item, dy = units[unit]
            chain(3, unit, True).wait_recv()
            chain(3, unit, False).wait_recv()
            summed[rows_of(unit), :] = (
                part[7, rows_of(unit), :] + up_in[3, rows_of(unit), :]
            ) + down_in[3, rows_of(unit), :]
            if item == 1:
                cross_copy(unit).start()
            else:

                @pl.when(h != w)
                def _():
                    cross_copy(unit).start()

                @pl.when(h == w)
                def _():
                    cross_in[h, dy] = summed[rows_of(unit), :]

    wave_copy.start()
    y_copies[0, True].start()
    y_copies[0, False].start()
    core_copies[0, 0].start()
    for d in range(2, Z):
        a_copies[d].start()
    for row in range(ROWS):
        row_blocks[row] = placed(looked[8 + row])
    own_rows[r] = row_blocks[r]
    split_ancestor(0)
    split_unit(0)
    y_copies[0, True].wait_recv()
    far_up.start()
    core_copies[0, 3].start()
    y_copies[0, False].wait_recv()
    core_copies[0, 1].start()
    wave_copy.wait_recv()
    y_copies[1, True].start()
    y_copies[1, False].start()
    core_copies[1, 0].start()
    split_unit(1)
    split_unit(2)
    split_unit(3)
    multiply(0, 0, 1)
    first_step(0)
    split_ancestor(1)
    split_ancestor(2)
    multiply(0, 1, 2)
    y_copies[1, False].wait_recv()
    far_down.start()
    core_copies[1, 1].start()
    y_copies[1, True].wait_recv()
    core_copies[1, 3].start()
    block_copies = []
    for offset in range(1, ROWS):
        other, device = row_peer(offset)
        copy = remote(
            row_blocks.at[other],
            own_rows.at[r],
            b_send.at[offset],
            b_recv.at[offset],
            **device,
        )
        copy.start()
        block_copies.append(copy)
    next_step(0, 1)
    far_up.wait_recv()
    core_copies[0, 2].start()
    split_ancestor(3)
    split_ancestor(4)
    multiply(0, 3, 2)
    split_unit(4)
    split_unit(5)
    split_unit(6)
    next_step(0, 2)
    far_down.wait_recv()
    core_copies[1, 2].start()
    split_unit(7)
    multiply(1, 0, 1)
    first_step(1)
    multiply(1, 1, 2)
    split_ancestor(5)
    split_ancestor(6)
    multiply(0, 5, 2)
    next_step(0, 3)
    next_step(1, 1)
    multiply(1, 3, 2)
    next_step(1, 2)
    multiply(1, 5, 2)
    split_ancestor(7)
    multiply(0, 7, 1)
    last_step(0)
    next_step(1, 3)
    multiply(1, 7, 1)
    last_step(1)

    for copy in block_copies:
        copy.wait_recv()

    for dy in (0, 1, 3, 2):
        for side in range(XH):

            @pl.when(jnp.logical_not(jnp.logical_and(h == w, h == side)))
            def _():
                remote(
                    summed.at[rows_of(0)],
                    cross_in.at[side, dy],
                    x_send.at[0],
                    x_recv.at[side, dy],
                    col_1=1 - h,
                ).wait_recv()

        squares = []
        for core in range(CORES):
            s = ((y + dy) % Y) * CORES + (k if core == 0 else 1 - k)
            rows = slice(core * W, (core + 1) * W)
            value = -(cross_in[0, dy, rows, :] + cross_in[1, dy, rows, :])
            value = jnp.where(held[s] > 0, value, jnp.zeros_like(value))
            panel_out[s] = value
            squares.append(dot_last(own_rows[s], value, HIGHEST))
        first = jnp.where(k == 0, squares[0], squares[1])
        update[(y + dy) % Y, :, :W] = first
        update[(y + dy) % Y, :, W:] = jnp.where(k == 0, squares[1], squares[0])

    def share(row, side):
        start = (row % CORES) * 32 + side * 16
        return pl.ds(pl.multiple_of(start, 16), 16)

    u_copies = []
    for offset in range(1, ROWS * XH):
        other, side, device = side_peer(offset)
        copy = remote(
            update.at[other // CORES, share(other, side)],
            row_in.at[offset],
            u_send.at[offset],
            u_recv.at[offset],
            **device,
        )
        copy.start()
        u_copies.append(copy)
    mine = share(r, h)
    partial = update[y, mine, :]
    for offset in range(1, ROWS * XH):
        u_copies[offset - 1].wait_recv()
        partial = partial + row_in[offset]
    col_in[0] = partial
    v_copies = []
    for offset in (4, 3, 5, 2, 6, 1, 7):
        copy = remote(
            col_in.at[0],
            col_in.at[offset],
            v_send.at[offset],
            v_recv.at[offset],
            col_0=(z + offset) % Z,
        )
        copy.start()
        v_copies.append(copy)
    for copy in v_copies:
        copy.wait_recv()
    whole = col_in[z]
    for owner in range(1, Z):
        whole = whole + col_in[(z + Z - owner) % Z]
    total[y, mine, :] = whole
    t_copies = []
    for offset in range(1, ROWS * XH):
        copy = remote(
            total.at[y, mine],
            total.at[y, mine],
            t_send.at[offset],
            t_recv.at[offset],
            **side_peer(offset)[2],
        )
        copy.start()
        t_copies.append(copy)
    for copy in t_copies:
        copy.wait_recv()
    for s in range(ROWS):
        lanes = slice((s % 2) * W, (s % 2 + 1) * W)
        block_out[s] = block_out[s] - total[s // 2, :, lanes]

    trade.wait_send()
    for copy in gathers.values():
        copy.wait_send()
    for copy in a_copies:
        copy.wait_send()
    wave_copy.wait_send()
    for copy in y_copies.values():
        copy.wait_send()
    for copy in core_copies.values():
        copy.wait_send()
    far_up.wait_send()
    far_down.wait_send()
    for copy in chains + block_copies + u_copies + v_copies + t_copies:
        copy.wait_send()
    for unit in range(8):
        if units[unit][0] == 1:
            cross_copy(unit).wait_send()
        else:

            @pl.when(h != w)
            def _():
                cross_copy(unit).wait_send()


def finish(panel_in, block_in, panel_out, block_out):
    panel_out[...] = panel_in[...]
    block_out[...] = block_in[...]


def per_device(lower_panel, diag_inverse, ancestor_inverse, pattern):
    ancestor = ancestor_inverse.reshape(Z, XH, BLK, HALF)
    vmem = pl.BlockSpec(memory_space=pltpu.VMEM)
    hbm = pl.BlockSpec(memory_space=pl.ANY)
    dma = pltpu.SemaphoreType.DMA
    sibs = WAVES * ROWS * W
    outs = (
        jax.ShapeDtypeStruct((ROWS, W, BLK), F32),
        jax.ShapeDtypeStruct((ROWS, W, W), F32),
    )
    panel, block = pl.pallas_call(
        kernel,
        out_shape=outs,
        in_specs=[pl.BlockSpec(memory_space=pltpu.SMEM), hbm, hbm, hbm],
        out_specs=(vmem, vmem),
        scratch_shapes=[
            pltpu.VMEM((W, 2 * BLK), F32),
            pltpu.VMEM((ROWS, W, W), F32),
            pltpu.VMEM((32, W, BLK), F32),
            pltpu.VMEM((WAVES * ROWS, W, KCOLS), F32),
            pltpu.VMEM((sibs, KCOLS), BF16),
            pltpu.VMEM((sibs, KCOLS), BF16),
            pltpu.VMEM((Z, WAVES, BLK, HALF), F32),
            pltpu.VMEM((Z, BLK, KCOLS), BF16),
            pltpu.VMEM((Z, BLK, KCOLS), BF16),
            pltpu.VMEM((Z, sibs, BLK), F32),
            pltpu.VMEM((4, sibs, BLK), F32),
            pltpu.VMEM((4, sibs, BLK), F32),
            pltpu.VMEM((sibs, BLK), F32),
            pltpu.VMEM((XH, Y, 2 * W, BLK), F32),
            pltpu.VMEM((ROWS, W, BLK), F32),
            pltpu.VMEM((ROWS, W, BLK), F32),
            pltpu.VMEM((Y, W, BLK), F32),
            pltpu.VMEM((ROWS * XH, 16, BLK), F32),
            pltpu.VMEM((Z, 16, BLK), F32),
            pltpu.VMEM((Y, W, BLK), F32),
            pltpu.SMEM((ROWS,), jnp.int32),
            dma((2,)),
            dma((Z,)),
            dma((Z,)),
            dma((Z,)),
            dma((2,)),
            dma((8,)),
            dma((8,)),
            dma((8,)),
            dma((8,)),
            dma((2,)),
            dma((4,)),
            dma((4,)),
            dma((2,)),
            dma((2,)),
            dma((8,)),
            dma((8,)),
            dma((ROWS,)),
            dma((ROWS,)),
            dma((4, 8)),
            dma((4, 8)),
            dma((4, 8)),
            dma((4, 8)),
            dma((8,)),
            dma((2, 4)),
            dma((ROWS * XH,)),
            dma((ROWS * XH,)),
            dma((Z,)),
            dma((Z,)),
            dma((ROWS * XH,)),
            dma((ROWS * XH,)),
        ],
        compiler_params=pltpu.CompilerParams(
            collective_id=0, has_side_effects=True, vmem_limit_bytes=60 * 1024 * 1024
        ),
        name="wave",
    )(pattern, lower_panel, diag_inverse, ancestor)
    return pl.pallas_call(
        finish,
        out_shape=outs,
        in_specs=[vmem, vmem],
        out_specs=(vmem, vmem),
        name="finish",
    )(panel, block)


def solution(mesh):
    finer = Mesh(
        mesh.devices.reshape(Y, CORES, Z, XH, WAVES),
        ("row_0", "row_1", "col_0", "col_1", "wave"),
    )
    placed = (P("wave", None, COL), P("wave", None, None), P(ROW, COL_WAVE), P("wave", None))
    return jax.shard_map(
        per_device,
        mesh=finer,
        in_specs=placed,
        out_specs=(P("wave", None, ROW_COL), P("wave", None, None)),
        check_vma=False,
    )
```

time: 151 us -> 113 us (0.75)
  Pallas kernels: 145 us -> 112 us
  local copies, waits for them, and re-layouts: 3.34 us -> 0 us
    pallas_call x1 -> x2, Pallas kernels: 145 us -> 112 us  [the longest x1 110 us: per_device(): pl.pallas_call(kernel, out_shape=outs, in_specs=[pl.BlockSpec(memory_spac...]
    unnamed x2 -> x0, local copies, waits for them, and re-layouts: 3.34 us -> none
where the time goes in v2:
time: 113 us
  Pallas kernels  112 us (99%)
    pallas_call x1, Pallas kernels, per_device(): pl.pallas_call(kernel, out_shape=outs, in_specs=[pl.BlockSpec(memory_spac...  110 us

profile of v2, /device:TPU:1, one launch (start us, length us, event | category | flops | bytes accessed | tf_op | source)
XLA Modules:
  0.0 112.8 jit_solution(16322896337943582232)
XLA Ops:
  0.6 110.3 %wave.1 = (f32[8,64,128]{2,1,0:T(8,128)}, f32[8,64,64]{2,1,0:T(8,128)}) custom-call(s32[8,32]{1,0:T(8,128)} %pattern.1, f32[8,64,256]{2,1,0:T(8,128)} %lower_hbm.1, f32[8,64,64]{2,1,0:T(8,128)} %diag_hbm.1, f32[8,2,128,512]{3,2,1,0:T(8,128)} %bitcast.1), custom_call_target="tpu_custom_call" | custom-call | tf_op jit(solution)/shard_map/wave/pallas_call | solution.py:565
  111.0 1.8 %finish.1 = (f32[8,64,128]{2,1,0:T(8,128)}, f32[8,64,64]{2,1,0:T(8,128)}) custom-call(f32[8,64,128]{2,1,0:T(8,128)} %get-tuple-element.4.panel_in, f32[8,64,64]{2,1,0:T(8,128)} %get-tuple-element.5.block_in), custom_call_target="tpu_custom_call" | custom-call | tf_op jit(solution)/shard_map/finish/pallas_call | solution.py:628

commit v3 on v2

--- a/solution.py
+++ b/solution.py
@@ -134,8 +134,6 @@
 
     take_lower = pltpu.make_async_copy(lower_hbm.at[r], lower, in_sem.at[0])
     take_diag = pltpu.make_async_copy(diag_hbm, diag, in_sem.at[1])
-    take_lower.start()
-    take_diag.start()
     for offset in range(1, Z):
         greet({"col_0": (z + offset) % Z})
     for offset in range(1, ROWS * XH):
@@ -143,6 +141,8 @@
     greet({"wave": 1 - w})
     greet({"col_1": 1 - h, "wave": 1 - w})
 
+    take_lower.start()
+    take_diag.start()
     places = [(z + offset) % Z for offset in (4, 3, 5, 2, 6, 1, 7, 0)]
     local = [
         pltpu.make_async_copy(ancestor.at[places[d], w], abuf.at[d, w], a_loc.at[d])
@@ -157,21 +157,6 @@
     packed[slot] = normed[:, :BLK]
     packed[slot + 1] = normed[:, BLK:]
 
-    own_block = r * COLS + c
-    wanted = [8 * c + j for j in range(8)] + [row * COLS + c for row in range(ROWS)]
-
-    def look(m, carry):
-        block = pattern[r, m]
-        found = [jnp.where(block == goal, m + 1, old) for goal, old in zip(wanted, carry[:16])]
-        kept = [
-            jnp.where(pattern[s, m] == own_block, 1, old) for s, old in enumerate(carry[16:])
-        ]
-        return tuple(found + kept)
-
-    looked = lax.fori_loop(0, 32, look, (jnp.int32(0),) * 24)
-    for s in range(ROWS):
-        held[s] = looked[16 + s]
-
     pl.semaphore_wait(barrier, 2 + (ROWS * XH - 1) + (Z - 1))
 
     def pair_at(place, side):
@@ -205,6 +190,23 @@
             view, view, send.at[slot_id], recv.at[slot_id], col_0=z_up if up else z_down
         )
 
+    own_block = r * COLS + c
+    wanted = [8 * c + j for j in range(8)] + [row * COLS + c for row in range(ROWS)]
+
+    def look(m, carry):
+        block = pattern[r, m]
+        found = [jnp.where(block == goal, m + 1, old) for goal, old in zip(wanted, carry[:16])]
+        kept = [
+            jnp.where(pattern[s, m] == own_block, 1, old) for s, old in enumerate(carry[16:])
+        ]
+        return tuple(found + kept)
+
+    def look_up():
+        looked = lax.fori_loop(0, 32, look, (jnp.int32(0),) * 24)
+        for s in range(ROWS):
+            held[s] = looked[16 + s]
+        return looked
+
     gathers = {}
     for step in range(1, 5):
         for own in range(2):
@@ -216,10 +218,13 @@
                 copy = z_gather(step, own, up)
                 copy.start()
                 gathers[step, own, up] = copy
-        if step <= 2:
+        if step <= 3:
             a_copies[step - 1].start()
-    for s in range(ROWS):
-        block_out[s] = dot_first(diag[s], diag[s])
+        if step == 1:
+            looked = look_up()
+        if step == 2:
+            for s in range(ROWS):
+                block_out[s] = dot_first(diag[s], diag[s])
     for own in range(2):
         for up in (True, False):
             gathers[4, own, up].wait_recv()
@@ -261,10 +266,23 @@
     wave_copy = spread((0, 0, 0), (1, 0, 0), w_sem.at[0], w_sem.at[1], wave=1 - w)
     y_copies = {(item, up): y_copy(item, up) for item in range(2) for up in (True, False)}
     core_copies = {(item, dy): core_copy(item, dy) for item in range(2) for dy in range(Y)}
-    far_up = spread((0, 3, 0), (0, 2, 0), f_send.at[0], f_recv.at[0], row_0=y_up)
-    far_down = spread((1, 1, 0), (1, 2, 0), f_send.at[1], f_recv.at[1], row_0=y_down)
+
+    def far_copy(item, up):
+        source = dense.at[spot(item, 3 if up else 1, 0), pl.ds(0 if up else W // 2, W // 2)]
+        target = dense.at[spot(item, 2, 0), pl.ds(0 if up else W // 2, W // 2)]
+        slot_id = 2 * item + (0 if up else 1)
+        return remote(
+            source,
+            target,
+            f_send.at[slot_id],
+            f_recv.at[slot_id],
+            row_0=y_up if up else y_down,
+        )
+
+    far_copies = {(item, up): far_copy(item, up) for item in range(2) for up in (True, False)}
 
     units = ((0, 0), (0, 1), (0, 3), (1, 0), (0, 2), (1, 1), (1, 3), (1, 2))
+    groups = (range(0, 3), range(3, 5), range(5, 8))
 
     def split_unit(unit):
         item, dy = units[unit]
@@ -286,14 +304,13 @@
     def multiply(group, first, count):
         right_hi = a_hi[first : first + count].reshape(count * BLK, KCOLS)
         right_lo = a_lo[first : first + count].reshape(count * BLK, KCOLS)
-        for start in range(group * 512, group * 512 + 512, 256):
-            rows = slice(start, start + 256)
-            left_hi, left_lo = dense_hi[rows, :], dense_lo[rows, :]
-            product = (
-                dot_last(left_hi, right_lo) + dot_last(left_lo, right_hi)
-            ) + dot_last(left_hi, right_hi)
-            for d in range(count):
-                part[first + d, rows, :] = product[:, d * BLK : (d + 1) * BLK]
+        rows = slice(groups[group][0] * BLK, (groups[group][-1] + 1) * BLK)
+        left_hi, left_lo = dense_hi[rows, :], dense_lo[rows, :]
+        product = (
+            dot_last(left_hi, right_lo) + dot_last(left_lo, right_hi)
+        ) + dot_last(left_hi, right_hi)
+        for d in range(count):
+            part[first + d, rows, :] = product[:, d * BLK : (d + 1) * BLK]
 
     def rows_of(unit):
         return pl.ds(unit * BLK, BLK)
@@ -317,11 +334,11 @@
         chains.append(copy)
 
     def first_step(group):
-        for unit in range(4 * group, 4 * group + 4):
+        for unit in groups[group]:
             send_on(0, unit, unit % 2 == 0)
 
     def next_step(group, t):
-        for unit in range(4 * group, 4 * group + 4):
+        for unit in groups[group]:
             for up in (True, False):
                 if t > 1 or (unit % 2 == 0) == up:
                     chain(t - 1, unit, up).wait_recv()
@@ -344,7 +361,7 @@
         )
 
     def last_step(group):
-        for unit in range(4 * group, 4 * group + 4):
+        for unit in groups[group]:
             item, dy = units[unit]
             chain(3, unit, True).wait_recv()
             chain(3, unit, False).wait_recv()
@@ -367,35 +384,45 @@
     y_copies[0, True].start()
     y_copies[0, False].start()
     core_copies[0, 0].start()
-    for d in range(2, Z):
+    for d in range(3, Z):
         a_copies[d].start()
     for row in range(ROWS):
         row_blocks[row] = placed(looked[8 + row])
     own_rows[r] = row_blocks[r]
     split_ancestor(0)
+    split_ancestor(1)
     split_unit(0)
     y_copies[0, True].wait_recv()
-    far_up.start()
+    far_copies[0, True].start()
     core_copies[0, 3].start()
     y_copies[0, False].wait_recv()
+    far_copies[0, False].start()
     core_copies[0, 1].start()
+    split_unit(1)
+    split_unit(2)
+    multiply(0, 0, 1)
+    first_step(0)
     wave_copy.wait_recv()
     y_copies[1, True].start()
     y_copies[1, False].start()
     core_copies[1, 0].start()
-    split_unit(1)
-    split_unit(2)
-    split_unit(3)
-    multiply(0, 0, 1)
-    first_step(0)
-    split_ancestor(1)
     split_ancestor(2)
     multiply(0, 1, 2)
+    for up in (True, False):
+        far_copies[0, up].wait_recv()
+    core_copies[0, 2].start()
+    next_step(0, 1)
+    split_unit(3)
+    split_unit(4)
+    multiply(1, 0, 1)
+    first_step(1)
+    multiply(1, 1, 2)
+    y_copies[1, True].wait_recv()
+    far_copies[1, True].start()
+    core_copies[1, 3].start()
     y_copies[1, False].wait_recv()
-    far_down.start()
+    far_copies[1, False].start()
     core_copies[1, 1].start()
-    y_copies[1, True].wait_recv()
-    core_copies[1, 3].start()
     block_copies = []
     for offset in range(1, ROWS):
         other, device = row_peer(offset)
@@ -408,36 +435,40 @@
         )
         copy.start()
         block_copies.append(copy)
-    next_step(0, 1)
-    far_up.wait_recv()
-    core_copies[0, 2].start()
+    next_step(1, 1)
     split_ancestor(3)
     split_ancestor(4)
     multiply(0, 3, 2)
-    split_unit(4)
+    next_step(0, 2)
+    multiply(1, 3, 2)
     split_unit(5)
     split_unit(6)
-    next_step(0, 2)
-    far_down.wait_recv()
+    next_step(1, 2)
+    for up in (True, False):
+        far_copies[1, up].wait_recv()
     core_copies[1, 2].start()
     split_unit(7)
-    multiply(1, 0, 1)
-    first_step(1)
-    multiply(1, 1, 2)
+    multiply(2, 0, 1)
+    first_step(2)
+    multiply(2, 1, 2)
+    next_step(2, 1)
     split_ancestor(5)
     split_ancestor(6)
     multiply(0, 5, 2)
     next_step(0, 3)
-    next_step(1, 1)
-    multiply(1, 3, 2)
-    next_step(1, 2)
     multiply(1, 5, 2)
+    next_step(1, 3)
+    multiply(2, 3, 2)
+    next_step(2, 2)
+    multiply(2, 5, 2)
     split_ancestor(7)
     multiply(0, 7, 1)
+    multiply(1, 7, 1)
     last_step(0)
-    next_step(1, 3)
-    multiply(1, 7, 1)
+    multiply(2, 7, 1)
     last_step(1)
+    next_step(2, 3)
+    last_step(2)
 
     for copy in block_copies:
         copy.wait_recv()
@@ -533,8 +564,8 @@
         copy.wait_send()
     for copy in core_copies.values():
         copy.wait_send()
-    far_up.wait_send()
-    far_down.wait_send()
+    for copy in far_copies.values():
+        copy.wait_send()
     for copy in chains + block_copies + u_copies + v_copies + t_copies:
         copy.wait_send()
     for unit in range(8):
@@ -545,11 +576,6 @@
             @pl.when(h != w)
             def _():
                 cross_copy(unit).wait_send()
-
-
-def finish(panel_in, block_in, panel_out, block_out):
-    panel_out[...] = panel_in[...]
-    block_out[...] = block_in[...]
 
 
 def per_device(lower_panel, diag_inverse, ancestor_inverse, pattern):
@@ -562,9 +588,9 @@
         jax.ShapeDtypeStruct((ROWS, W, BLK), F32),
         jax.ShapeDtypeStruct((ROWS, W, W), F32),
     )
-    panel, block = pl.pallas_call(
+    return pl.pallas_call(
         kernel,
-        out_shape=outs,
+        out_shape=tuple(pltpu.VMEM(out.shape, out.dtype) for out in outs),
         in_specs=[pl.BlockSpec(memory_space=pltpu.SMEM), hbm, hbm, hbm],
         out_specs=(vmem, vmem),
         scratch_shapes=[
@@ -601,8 +627,8 @@
             dma((2,)),
             dma((4,)),
             dma((4,)),
-            dma((2,)),
-            dma((2,)),
+            dma((4,)),
+            dma((4,)),
             dma((8,)),
             dma((8,)),
             dma((ROWS,)),
@@ -625,13 +651,6 @@
         ),
         name="wave",
     )(pattern, lower_panel, diag_inverse, ancestor)
-    return pl.pallas_call(
-        finish,
-        out_shape=outs,
-        in_specs=[vmem, vmem],
-        out_specs=(vmem, vmem),
-        name="finish",
-    )(panel, block)
 
 
 def solution(mesh):

time: 113 us -> 110 us (0.973)
  Pallas kernels: 112 us -> 107 us
  local copies, waits for them, and re-layouts: 0 us -> 1.41 us
    pallas_call x2 -> x1, Pallas kernels: 112 us -> 107 us  [per_device(): pl.pallas_call(kernel, out_shape=tuple((pltpu.VMEM(out.shape, out.dtype)...]
    unnamed x0 -> x2, local copies, waits for them, and re-layouts: none -> 1.41 us
where the time goes in v3:
time: 110 us
  Pallas kernels  107 us (97%)
  local copies, waits for them, and re-layouts  1.41 us (1%)
    pallas_call x1, Pallas kernels, per_device(): pl.pallas_call(kernel, out_shape=tuple((pltpu.VMEM(out.shape, out.dtype)...  107 us

profile of v3, /device:TPU:1, one launch (start us, length us, event | category | flops | bytes accessed | tf_op | source)
XLA Modules:
  0.0 109.5 jit_solution(9959246713405209834)
XLA Ops:
  0.6 107.5 %wave.1 = (f32[8,64,128]{2,1,0:T(8,128)S(1)}, f32[8,64,64]{2,1,0:T(8,128)S(1)}) custom-call(s32[8,32]{1,0:T(8,128)} %pattern.1, f32[8,64,256]{2,1,0:T(8,128)} %lower_hbm.1, f32[8,64,64]{2,1,0:T(8,128)} %diag_hbm.1, f32[8,2,128,512]{3,2,1,0:T(8,128)} %bitcast.1), custom_call_target="tpu_custom_call" | custom-call | tf_op jit(solution)/shard_map/wave/pallas_call | solution.py:591
  108.1 0.7 copy.8
  108.8 0.7 copy.9

commit v4 on v3

--- a/solution.py
+++ b/solution.py
@@ -8,6 +8,7 @@
 
 W = 64
 BLK = 128
+PART = 32
 Y, CORES, Z, XH, WAVES = 4, 2, 8, 2, 2
 ROWS = Y * CORES
 COLS = Z * XH
@@ -60,8 +61,10 @@
     block_out,
     lower,
     diag,
-    packed,
-    dense,
+    packed_a,
+    packed_b,
+    dense_a,
+    dense_b,
     dense_hi,
     dense_lo,
     abuf,
@@ -117,6 +120,7 @@
     w = lax.axis_index("wave")
     r = y * CORES + k
     c = z * XH + h
+    packed, dense = (packed_a, packed_b), (dense_a, dense_b)
 
     def row_peer(offset):
         other = (r + offset) % ROWS
@@ -134,12 +138,11 @@
 
     take_lower = pltpu.make_async_copy(lower_hbm.at[r], lower, in_sem.at[0])
     take_diag = pltpu.make_async_copy(diag_hbm, diag, in_sem.at[1])
-    for offset in range(1, Z):
-        greet({"col_0": (z + offset) % Z})
-    for offset in range(1, ROWS * XH):
-        greet(side_peer(offset)[2])
-    greet({"wave": 1 - w})
-    greet({"col_1": 1 - h, "wave": 1 - w})
+    near = [{"col_0": (z + 1) % Z}, {"col_0": (z + Z - 1) % Z}, {"col_1": 1 - h}]
+    near += [{"row_0": (y + 1) % Y}, {"row_0": (y + Y - 1) % Y}, {"row_1": 1 - k}]
+    near += [{"wave": 1 - w}]
+    for device in near:
+        greet(device)
 
     take_lower.start()
     take_diag.start()
@@ -154,16 +157,21 @@
     take_diag.wait()
     normed = dot_first(diag[r], lower[...])
     slot = 2 * c
-    packed[slot] = normed[:, :BLK]
-    packed[slot + 1] = normed[:, BLK:]
-
-    pl.semaphore_wait(barrier, 2 + (ROWS * XH - 1) + (Z - 1))
-
-    def pair_at(place, side):
-        return packed.at[pl.ds(2 * (place * XH + side), 2)]
-
-    trade = remote(pair_at(z, h), pair_at(z, h), h_sem.at[0], h_sem.at[1], col_1=1 - h)
-    trade.start()
+    for g in range(2):
+        packed[g][slot] = normed[g * PART : (g + 1) * PART, :BLK]
+        packed[g][slot + 1] = normed[g * PART : (g + 1) * PART, BLK:]
+
+    pl.semaphore_wait(barrier, len(near))
+
+    def pair_at(g, place, side):
+        return packed[g].at[pl.ds(2 * (place * XH + side), 2)]
+
+    trades = []
+    for g in range(2):
+        own_pair = pair_at(g, z, h)
+        trade = remote(own_pair, own_pair, h_sem.at[2 * g], h_sem.at[2 * g + 1], col_1=1 - h)
+        trade.start()
+        trades.append(trade)
 
     a_copies = [
         remote(
@@ -177,15 +185,15 @@
     ]
     z_up, z_down = (z + 1) % Z, (z + Z - 1) % Z
 
-    def z_gather(step, own, up):
+    def z_gather(step, own, g, up):
         side = h if own == 0 else 1 - h
         source = (z + Z - (step - 1)) % Z if up else (z + step - 1) % Z
         if step < 4:
-            view = pair_at(source, side)
+            view = pair_at(g, source, side)
         else:
-            view = packed.at[pl.ds(2 * (source * XH + side) + (0 if up else 1), 1)]
+            view = packed[g].at[pl.ds(2 * (source * XH + side) + (0 if up else 1), 1)]
         send, recv = (zp_send, zp_recv) if up else (zm_send, zm_recv)
-        slot_id = 2 * (step - 1) + own
+        slot_id = 4 * (step - 1) + 2 * own + g
         return remote(
             view, view, send.at[slot_id], recv.at[slot_id], col_0=z_up if up else z_down
         )
@@ -209,47 +217,53 @@
 
     gathers = {}
     for step in range(1, 5):
-        for own in range(2):
+        if step == 1:
+            pieces = ((0, 0), (0, 1), (1, 0), (1, 1))
+        else:
+            pieces = ((0, 0), (1, 0), (0, 1), (1, 1))
+        for own, g in pieces:
             if step == 1 and own == 1:
-                trade.wait_recv()
+                trades[g].wait_recv()
             for up in (True, False):
                 if step > 1:
-                    gathers[step - 1, own, up].wait_recv()
-                copy = z_gather(step, own, up)
+                    gathers[step - 1, own, g, up].wait_recv()
+                copy = z_gather(step, own, g, up)
                 copy.start()
-                gathers[step, own, up] = copy
-        if step <= 3:
+                gathers[step, own, g, up] = copy
+        if step <= 2:
             a_copies[step - 1].start()
         if step == 1:
             looked = look_up()
         if step == 2:
             for s in range(ROWS):
                 block_out[s] = dot_first(diag[s], diag[s])
-    for own in range(2):
-        for up in (True, False):
-            gathers[4, own, up].wait_recv()
-
-    def placed(found):
-        value = packed[jnp.maximum(found - 1, 0)]
+
+    def placed(found, g):
+        value = packed[g][jnp.maximum(found - 1, 0)]
         return jnp.where(found > 0, value, jnp.zeros_like(value))
 
-    for j in range(8):
-        dense[0, :, j * BLK : (j + 1) * BLK] = placed(looked[j])
+    def place(g):
+        for own in range(2):
+            for up in (True, False):
+                gathers[4, own, g, up].wait_recv()
+        for j in range(8):
+            dense[g][0, :, j * BLK : (j + 1) * BLK] = placed(looked[j], g)
 
     def spot(item, dy, core):
         return (item * Y + dy) * CORES + core
 
-    def spread(source, target, send, recv, **device):
+    def spread(g, source, target, send, recv, **device):
         return remote(
-            dense.at[spot(*source)], dense.at[spot(*target)], send, recv, **device
+            dense[g].at[spot(*source)], dense[g].at[spot(*target)], send, recv, **device
         )
 
     y_up, y_down = (y + 1) % Y, (y + Y - 1) % Y
     waves = (w, 1 - w)
 
-    def y_copy(item, up):
-        slot_id = 2 * item + (0 if up else 1)
+    def y_copy(g, item, up):
+        slot_id = 4 * g + 2 * item + (0 if up else 1)
         return spread(
+            g,
             (item, 0, 0),
             (item, 3 if up else 1, 0),
             y_send.at[slot_id],
@@ -257,41 +271,62 @@
             row_0=y_up if up else y_down,
         )
 
-    def core_copy(item, dy):
-        slot_id = 4 * item + dy
+    def core_copy(g, item, dy):
+        slot_id = 8 * g + 4 * item + dy
         return spread(
-            (item, dy, 0), (item, dy, 1), c_send.at[slot_id], c_recv.at[slot_id], row_1=1 - k
-        )
-
-    wave_copy = spread((0, 0, 0), (1, 0, 0), w_sem.at[0], w_sem.at[1], wave=1 - w)
-    y_copies = {(item, up): y_copy(item, up) for item in range(2) for up in (True, False)}
-    core_copies = {(item, dy): core_copy(item, dy) for item in range(2) for dy in range(Y)}
-
-    def far_copy(item, up):
-        source = dense.at[spot(item, 3 if up else 1, 0), pl.ds(0 if up else W // 2, W // 2)]
-        target = dense.at[spot(item, 2, 0), pl.ds(0 if up else W // 2, W // 2)]
-        slot_id = 2 * item + (0 if up else 1)
+            g, (item, dy, 0), (item, dy, 1), c_send.at[slot_id], c_recv.at[slot_id], row_1=1 - k
+        )
+
+    def far_copy(g, item, up):
+        rows = pl.ds(0 if up else PART // 2, PART // 2)
+        slot_id = 4 * g + 2 * item + (0 if up else 1)
         return remote(
-            source,
-            target,
+            dense[g].at[spot(item, 3 if up else 1, 0), rows],
+            dense[g].at[spot(item, 2, 0), rows],
             f_send.at[slot_id],
             f_recv.at[slot_id],
             row_0=y_up if up else y_down,
         )
 
-    far_copies = {(item, up): far_copy(item, up) for item in range(2) for up in (True, False)}
-
-    units = ((0, 0), (0, 1), (0, 3), (1, 0), (0, 2), (1, 1), (1, 3), (1, 2))
-    groups = (range(0, 3), range(3, 5), range(5, 8))
-
-    def split_unit(unit):
-        item, dy = units[unit]
-        core_copies[item, dy].wait_recv()
-        for core in range(CORES):
-            rows = slice(unit * BLK + core * W, unit * BLK + (core + 1) * W)
-            high, low = halves(dense[spot(item, dy, core)])
-            dense_hi[rows, :] = high
-            dense_lo[rows, :] = low
+    both = [(g, item) for g in range(2) for item in range(2)]
+    wave_copies = [
+        spread(g, (0, 0, 0), (1, 0, 0), w_sem.at[2 * g], w_sem.at[2 * g + 1], wave=1 - w)
+        for g in range(2)
+    ]
+    y_copies = {(*at, up): y_copy(*at, up) for at in both for up in (True, False)}
+    far_copies = {(*at, up): far_copy(*at, up) for at in both for up in (True, False)}
+    core_copies = {(*at, dy): core_copy(*at, dy) for at in both for dy in range(Y)}
+
+    order = (0, 1, 3, 2)
+    groups = (range(0, 2), range(2, 4), range(4, 6), range(6, 8))
+
+    def kind(unit):
+        return unit // 2 % 2, unit // 4, unit % 2
+
+    def start_y(g, item):
+        y_copies[g, item, True].start()
+        y_copies[g, item, False].start()
+        core_copies[g, item, 0].start()
+
+    def start_far(g, item):
+        for up, dy in ((True, 3), (False, 1)):
+            y_copies[g, item, up].wait_recv()
+            far_copies[g, item, up].start()
+            core_copies[g, item, dy].start()
+
+    def end_far(g, item):
+        for up in (True, False):
+            far_copies[g, item, up].wait_recv()
+        core_copies[g, item, 2].start()
+
+    def split(g, item, dys):
+        for dy in dys:
+            core_copies[g, item, dy].wait_recv()
+            for core in range(CORES):
+                start = (2 * item + g) * 256 + order.index(dy) * W + core * PART
+                high, low = halves(dense[g][spot(item, dy, core)])
+                dense_hi[start : start + PART, :] = high
+                dense_lo[start : start + PART, :] = low
 
     def split_ancestor(d):
         local[d].wait()
@@ -350,19 +385,19 @@
                 send_on(t, unit, up)
 
     def cross_copy(unit):
-        item, dy = units[unit]
+        g, item, pair = kind(unit)
         return remote(
             summed.at[rows_of(unit)],
-            cross_in.at[h, dy],
+            cross_in.at[h, 2 * g + pair],
             x_send.at[unit],
-            x_recv.at[h, dy],
+            x_recv.at[h, 2 * g + pair],
             col_1=w,
             wave=waves[item],
         )
 
     def last_step(group):
         for unit in groups[group]:
-            item, dy = units[unit]
+            g, item, pair = kind(unit)
             chain(3, unit, True).wait_recv()
             chain(3, unit, False).wait_recv()
             summed[rows_of(unit), :] = (
@@ -378,51 +413,55 @@
 
                 @pl.when(h == w)
                 def _():
-                    cross_in[h, dy] = summed[rows_of(unit), :]
-
-    wave_copy.start()
-    y_copies[0, True].start()
-    y_copies[0, False].start()
-    core_copies[0, 0].start()
-    for d in range(3, Z):
-        a_copies[d].start()
+                    cross_in[h, 2 * g + pair] = summed[rows_of(unit), :]
+
+    place(0)
+    wave_copies[0].start()
+    start_y(0, 0)
+    place(1)
+    wave_copies[1].start()
+    start_y(1, 0)
     for row in range(ROWS):
-        row_blocks[row] = placed(looked[8 + row])
+        for g in range(2):
+            row_blocks[row, g * PART : (g + 1) * PART, :] = placed(looked[8 + row], g)
     own_rows[r] = row_blocks[r]
     split_ancestor(0)
     split_ancestor(1)
-    split_unit(0)
-    y_copies[0, True].wait_recv()
-    far_copies[0, True].start()
-    core_copies[0, 3].start()
-    y_copies[0, False].wait_recv()
-    far_copies[0, False].start()
-    core_copies[0, 1].start()
-    split_unit(1)
-    split_unit(2)
+    split(0, 0, (0,))
+    start_far(0, 0)
+    wave_copies[0].wait_recv()
+    start_y(0, 1)
+    a_copies[2].start()
+    split(0, 0, (1, 3))
+    start_far(1, 0)
+    wave_copies[1].wait_recv()
+    start_y(1, 1)
+    for d in range(3, Z):
+        a_copies[d].start()
+    end_far(0, 0)
+    split(1, 0, (0, 1, 3))
+    split(0, 0, (2,))
     multiply(0, 0, 1)
     first_step(0)
-    wave_copy.wait_recv()
-    y_copies[1, True].start()
-    y_copies[1, False].start()
-    core_copies[1, 0].start()
+    start_far(0, 1)
+    end_far(1, 0)
     split_ancestor(2)
     multiply(0, 1, 2)
-    for up in (True, False):
-        far_copies[0, up].wait_recv()
-    core_copies[0, 2].start()
-    next_step(0, 1)
-    split_unit(3)
-    split_unit(4)
+    split(1, 0, (2,))
     multiply(1, 0, 1)
     first_step(1)
+    next_step(0, 1)
     multiply(1, 1, 2)
-    y_copies[1, True].wait_recv()
-    far_copies[1, True].start()
-    core_copies[1, 3].start()
-    y_copies[1, False].wait_recv()
-    far_copies[1, False].start()
-    core_copies[1, 1].start()
+    start_far(1, 1)
+    split(0, 1, (0, 1, 3))
+    next_step(1, 1)
+    end_far(0, 1)
+    split(1, 1, (0, 1, 3))
+    split(0, 1, (2,))
+    multiply(2, 0, 1)
+    first_step(2)
+    multiply(2, 1, 2)
+    end_far(1, 1)
     block_copies = []
     for offset in range(1, ROWS):
         other, device = row_peer(offset)
@@ -435,67 +474,75 @@
         )
         copy.start()
         block_copies.append(copy)
-    next_step(1, 1)
+    split(1, 1, (2,))
+    multiply(3, 0, 1)
+    first_step(3)
+    next_step(2, 1)
+    multiply(3, 1, 2)
     split_ancestor(3)
     split_ancestor(4)
     multiply(0, 3, 2)
+    next_step(3, 1)
     next_step(0, 2)
     multiply(1, 3, 2)
-    split_unit(5)
-    split_unit(6)
     next_step(1, 2)
-    for up in (True, False):
-        far_copies[1, up].wait_recv()
-    core_copies[1, 2].start()
-    split_unit(7)
-    multiply(2, 0, 1)
-    first_step(2)
-    multiply(2, 1, 2)
-    next_step(2, 1)
+    multiply(2, 3, 2)
+    next_step(2, 2)
+    multiply(3, 3, 2)
     split_ancestor(5)
     split_ancestor(6)
     multiply(0, 5, 2)
     next_step(0, 3)
+    next_step(3, 2)
     multiply(1, 5, 2)
     next_step(1, 3)
-    multiply(2, 3, 2)
-    next_step(2, 2)
     multiply(2, 5, 2)
+    next_step(2, 3)
+    multiply(3, 5, 2)
     split_ancestor(7)
     multiply(0, 7, 1)
     multiply(1, 7, 1)
+    next_step(3, 3)
     last_step(0)
     multiply(2, 7, 1)
+    multiply(3, 7, 1)
     last_step(1)
-    next_step(2, 3)
     last_step(2)
+    last_step(3)
 
     for copy in block_copies:
         copy.wait_recv()
 
-    for dy in (0, 1, 3, 2):
+    def sibling(dy, core):
+        return ((y + dy) % Y) * CORES + (k if core == 0 else 1 - k)
+
+    for g, pair in ((0, 0), (0, 1), (1, 0), (1, 1)):
         for side in range(XH):
 
             @pl.when(jnp.logical_not(jnp.logical_and(h == w, h == side)))
             def _():
                 remote(
                     summed.at[rows_of(0)],
-                    cross_in.at[side, dy],
+                    cross_in.at[side, 2 * g + pair],
                     x_send.at[0],
-                    x_recv.at[side, dy],
+                    x_recv.at[side, 2 * g + pair],
                     col_1=1 - h,
                 ).wait_recv()
 
+        for index in range(2):
+            for core in range(CORES):
+                s = sibling(order[2 * pair + index], core)
+                rows = slice((2 * index + core) * PART, (2 * index + core + 1) * PART)
+                value = -(cross_in[0, 2 * g + pair, rows, :] + cross_in[1, 2 * g + pair, rows, :])
+                value = jnp.where(held[s] > 0, value, jnp.zeros_like(value))
+                panel_out[s, g * PART : (g + 1) * PART, :] = value
+
+    for dy in range(Y):
         squares = []
         for core in range(CORES):
-            s = ((y + dy) % Y) * CORES + (k if core == 0 else 1 - k)
-            rows = slice(core * W, (core + 1) * W)
-            value = -(cross_in[0, dy, rows, :] + cross_in[1, dy, rows, :])
-            value = jnp.where(held[s] > 0, value, jnp.zeros_like(value))
-            panel_out[s] = value
-            squares.append(dot_last(own_rows[s], value, HIGHEST))
-        first = jnp.where(k == 0, squares[0], squares[1])
-        update[(y + dy) % Y, :, :W] = first
+            s = sibling(dy, core)
+            squares.append(dot_last(own_rows[s], panel_out[s], HIGHEST))
+        update[(y + dy) % Y, :, :W] = jnp.where(k == 0, squares[0], squares[1])
         update[(y + dy) % Y, :, W:] = jnp.where(k == 0, squares[1], squares[0])
 
     def share(row, side):
@@ -554,12 +601,12 @@
         lanes = slice((s % 2) * W, (s % 2 + 1) * W)
         block_out[s] = block_out[s] - total[s // 2, :, lanes]
 
-    trade.wait_send()
+    for copy in trades + wave_copies:
+        copy.wait_send()
     for copy in gathers.values():
         copy.wait_send()
     for copy in a_copies:
         copy.wait_send()
-    wave_copy.wait_send()
     for copy in y_copies.values():
         copy.wait_send()
     for copy in core_copies.values():
@@ -569,7 +616,7 @@
     for copy in chains + block_copies + u_copies + v_copies + t_copies:
         copy.wait_send()
     for unit in range(8):
-        if units[unit][0] == 1:
+        if kind(unit)[1] == 1:
             cross_copy(unit).wait_send()
         else:
 
@@ -596,8 +643,10 @@
         scratch_shapes=[
             pltpu.VMEM((W, 2 * BLK), F32),
             pltpu.VMEM((ROWS, W, W), F32),
-            pltpu.VMEM((32, W, BLK), F32),
-            pltpu.VMEM((WAVES * ROWS, W, KCOLS), F32),
+            pltpu.VMEM((32, PART, BLK), F32),
+            pltpu.VMEM((32, PART, BLK), F32),
+            pltpu.VMEM((WAVES * ROWS, PART, KCOLS), F32),
+            pltpu.VMEM((WAVES * ROWS, PART, KCOLS), F32),
             pltpu.VMEM((sibs, KCOLS), BF16),
             pltpu.VMEM((sibs, KCOLS), BF16),
             pltpu.VMEM((Z, WAVES, BLK, HALF), F32),
@@ -619,18 +668,18 @@
             dma((Z,)),
             dma((Z,)),
             dma((Z,)),
-            dma((2,)),
+            dma((4,)),
+            dma((16,)),
+            dma((16,)),
+            dma((16,)),
+            dma((16,)),
+            dma((4,)),
             dma((8,)),
             dma((8,)),
             dma((8,)),
             dma((8,)),
-            dma((2,)),
-            dma((4,)),
-            dma((4,)),
-            dma((4,)),
-            dma((4,)),
-            dma((8,)),
-            dma((8,)),
+            dma((16,)),
+            dma((16,)),
             dma((ROWS,)),
             dma((ROWS,)),
             dma((4, 8)),

time: 110 us -> 108 us (0.982)
    pallas_call x1, Pallas kernels: 107 us -> 106 us  [per_device(): pl.pallas_call(kernel, out_shape=tuple((pltpu.VMEM(out.shape, out.dtype)...]
where the time goes in v4:
time: 108 us
  Pallas kernels  106 us (98%)
  local copies, waits for them, and re-layouts  1.41 us (1%)
    pallas_call x1, Pallas kernels, per_device(): pl.pallas_call(kernel, out_shape=tuple((pltpu.VMEM(out.shape, out.dtype)...  106 us

profile of v4, /device:TPU:1, one launch (start us, length us, event | category | flops | bytes accessed | tf_op | source)
XLA Modules:
  0.0 107.6 jit_solution(13233234354934038835)
XLA Ops:
  0.6 105.6 %wave.1 = (f32[8,64,128]{2,1,0:T(8,128)S(1)}, f32[8,64,64]{2,1,0:T(8,128)S(1)}) custom-call(s32[8,32]{1,0:T(8,128)} %pattern.1, f32[8,64,256]{2,1,0:T(8,128)} %lower_hbm.1, f32[8,64,64]{2,1,0:T(8,128)} %diag_hbm.1, f32[8,2,128,512]{3,2,1,0:T(8,128)} %bitcast.1), custom_call_target="tpu_custom_call" | custom-call | tf_op jit(solution)/shard_map/wave/pallas_call | solution.py:638
  106.2 0.7 copy.8
  106.9 0.7 copy.9

commit v5 on v4

--- a/solution.py
+++ b/solution.py
@@ -77,6 +77,8 @@
     cross_in,
     row_blocks,
     own_rows,
+    pass_rows,
+    far_rows,
     update,
     row_in,
     col_in,
@@ -100,6 +102,7 @@
     c_recv,
     b_send,
     b_recv,
+    p_sem,
     up_send,
     up_recv,
     down_send,
@@ -199,20 +202,22 @@
         )
 
     own_block = r * COLS + c
-    wanted = [8 * c + j for j in range(8)] + [row * COLS + c for row in range(ROWS)]
+    wanted = [8 * c + j for j in range(8)]
+    for parity in (w, 1 - w):
+        wanted += [row * COLS + z * XH + parity for row in range(ROWS)]
 
     def look(m, carry):
         block = pattern[r, m]
-        found = [jnp.where(block == goal, m + 1, old) for goal, old in zip(wanted, carry[:16])]
+        found = [jnp.where(block == goal, m + 1, old) for goal, old in zip(wanted, carry[:24])]
         kept = [
-            jnp.where(pattern[s, m] == own_block, 1, old) for s, old in enumerate(carry[16:])
+            jnp.where(pattern[s, m] == own_block, 1, old) for s, old in enumerate(carry[24:])
         ]
         return tuple(found + kept)
 
     def look_up():
-        looked = lax.fori_loop(0, 32, look, (jnp.int32(0),) * 24)
+        looked = lax.fori_loop(0, 32, look, (jnp.int32(0),) * 32)
         for s in range(ROWS):
-            held[s] = looked[16 + s]
+            held[s] = looked[24 + s]
         return looked
 
     gathers = {}
@@ -403,6 +408,10 @@
             summed[rows_of(unit), :] = (
                 part[7, rows_of(unit), :] + up_in[3, rows_of(unit), :]
             ) + down_in[3, rows_of(unit), :]
+
+    def start_cross(group):
+        for unit in groups[group]:
+            g, item, pair = kind(unit)
             if item == 1:
                 cross_copy(unit).start()
             else:
@@ -414,6 +423,42 @@
                 @pl.when(h == w)
                 def _():
                     cross_in[h, 2 * g + pair] = summed[rows_of(unit), :]
+
+    def sibling(dy, core):
+        return ((y + dy) % Y) * CORES + (k if core == 0 else 1 - k)
+
+    def share(row, side):
+        start = (row % CORES) * 32 + side * 16
+        return pl.ds(pl.multiple_of(start, 16), 16)
+
+    u_copies = {}
+
+    def start_update(item):
+        blocks = own_rows if item == 0 else far_rows
+        for dy in range(Y):
+            squares = []
+            for core in range(CORES):
+                start = item * 512 + order.index(dy) * W + core * PART
+                value = jnp.concatenate(
+                    [summed[start + g * 256 : start + g * 256 + PART, :] for g in range(2)], axis=0
+                )
+                squares.append(dot_last(blocks[sibling(dy, core)], value, HIGHEST))
+            update[item, (y + dy) % Y, :, :W] = jnp.where(k == 0, squares[0], squares[1])
+            update[item, (y + dy) % Y, :, W:] = jnp.where(k == 0, squares[1], squares[0])
+        for offset in range(1 - item, ROWS * XH):
+            other, side, device = side_peer(offset)
+            if item == 1:
+                device["wave"] = 1 - w
+            slot_id = item * ROWS * XH + offset
+            copy = remote(
+                update.at[item, other // CORES, share(other, side)],
+                row_in.at[slot_id],
+                u_send.at[slot_id],
+                u_recv.at[slot_id],
+                **device,
+            )
+            copy.start()
+            u_copies[slot_id] = copy
 
     place(0)
     wave_copies[0].start()
@@ -421,10 +466,11 @@
     place(1)
     wave_copies[1].start()
     start_y(1, 0)
-    for row in range(ROWS):
+    for place_id in range(2 * ROWS):
         for g in range(2):
-            row_blocks[row, g * PART : (g + 1) * PART, :] = placed(looked[8 + row], g)
+            row_blocks[place_id, g * PART : (g + 1) * PART, :] = placed(looked[8 + place_id], g)
     own_rows[r] = row_blocks[r]
+    pass_rows[r] = row_blocks[ROWS + r]
     split_ancestor(0)
     split_ancestor(1)
     split(0, 0, (0,))
@@ -463,17 +509,19 @@
     multiply(2, 1, 2)
     end_far(1, 1)
     block_copies = []
-    for offset in range(1, ROWS):
-        other, device = row_peer(offset)
-        copy = remote(
-            row_blocks.at[other],
-            own_rows.at[r],
-            b_send.at[offset],
-            b_recv.at[offset],
-            **device,
-        )
-        copy.start()
-        block_copies.append(copy)
+    for kept, into in enumerate((own_rows, pass_rows)):
+        for offset in range(1, ROWS):
+            other, device = row_peer(offset)
+            slot_id = kept * ROWS + offset
+            copy = remote(
+                row_blocks.at[kept * ROWS + other],
+                into.at[r],
+                b_send.at[slot_id],
+                b_recv.at[slot_id],
+                **device,
+            )
+            copy.start()
+            block_copies.append(copy)
     split(1, 1, (2,))
     multiply(3, 0, 1)
     first_step(3)
@@ -491,6 +539,10 @@
     multiply(3, 3, 2)
     split_ancestor(5)
     split_ancestor(6)
+    for copy in block_copies:
+        copy.wait_recv()
+    pass_copy = remote(pass_rows, far_rows, p_sem.at[0], p_sem.at[1], wave=1 - w)
+    pass_copy.start()
     multiply(0, 5, 2)
     next_step(0, 3)
     next_step(3, 2)
@@ -504,17 +556,36 @@
     multiply(1, 7, 1)
     next_step(3, 3)
     last_step(0)
+    start_cross(0)
     multiply(2, 7, 1)
     multiply(3, 7, 1)
     last_step(1)
+    start_cross(1)
+    start_update(0)
     last_step(2)
     last_step(3)
-
-    for copy in block_copies:
+    pass_copy.wait_recv()
+    start_update(1)
+    start_cross(2)
+    start_cross(3)
+
+    mine = share(r, h)
+    partial = update[0, y, mine, :]
+    for slot_id, copy in u_copies.items():
         copy.wait_recv()
-
-    def sibling(dy, core):
-        return ((y + dy) % Y) * CORES + (k if core == 0 else 1 - k)
+        partial = partial + row_in[slot_id]
+    col_in[0] = partial
+    v_copies = []
+    for offset in (4, 3, 5, 2, 6, 1, 7):
+        copy = remote(
+            col_in.at[0],
+            col_in.at[offset],
+            v_send.at[offset],
+            v_recv.at[offset],
+            col_0=(z + offset) % Z,
+        )
+        copy.start()
+        v_copies.append(copy)
 
     for g, pair in ((0, 0), (0, 1), (1, 0), (1, 1)):
         for side in range(XH):
@@ -537,47 +608,6 @@
                 value = jnp.where(held[s] > 0, value, jnp.zeros_like(value))
                 panel_out[s, g * PART : (g + 1) * PART, :] = value
 
-    for dy in range(Y):
-        squares = []
-        for core in range(CORES):
-            s = sibling(dy, core)
-            squares.append(dot_last(own_rows[s], panel_out[s], HIGHEST))
-        update[(y + dy) % Y, :, :W] = jnp.where(k == 0, squares[0], squares[1])
-        update[(y + dy) % Y, :, W:] = jnp.where(k == 0, squares[1], squares[0])
-
-    def share(row, side):
-        start = (row % CORES) * 32 + side * 16
-        return pl.ds(pl.multiple_of(start, 16), 16)
-
-    u_copies = []
-    for offset in range(1, ROWS * XH):
-        other, side, device = side_peer(offset)
-        copy = remote(
-            update.at[other // CORES, share(other, side)],
-            row_in.at[offset],
-            u_send.at[offset],
-            u_recv.at[offset],
-            **device,
-        )
-        copy.start()
-        u_copies.append(copy)
-    mine = share(r, h)
-    partial = update[y, mine, :]
-    for offset in range(1, ROWS * XH):
-        u_copies[offset - 1].wait_recv()
-        partial = partial + row_in[offset]
-    col_in[0] = partial
-    v_copies = []
-    for offset in (4, 3, 5, 2, 6, 1, 7):
-        copy = remote(
-            col_in.at[0],
-            col_in.at[offset],
-            v_send.at[offset],
-            v_recv.at[offset],
-            col_0=(z + offset) % Z,
-        )
-        copy.start()
-        v_copies.append(copy)
     for copy in v_copies:
         copy.wait_recv()
     whole = col_in[z]
@@ -599,9 +629,9 @@
         copy.wait_recv()
     for s in range(ROWS):
         lanes = slice((s % 2) * W, (s % 2 + 1) * W)
-        block_out[s] = block_out[s] - total[s // 2, :, lanes]
-
-    for copy in trades + wave_copies:
+        block_out[s] = block_out[s] + total[s // 2, :, lanes]
+
+    for copy in trades + wave_copies + [pass_copy] + list(u_copies.values()):
         copy.wait_send()
     for copy in gathers.values():
         copy.wait_send()
@@ -613,7 +643,7 @@
         copy.wait_send()
     for copy in far_copies.values():
         copy.wait_send()
-    for copy in chains + block_copies + u_copies + v_copies + t_copies:
+    for copy in chains + block_copies + v_copies + t_copies:
         copy.wait_send()
     for unit in range(8):
         if kind(unit)[1] == 1:
@@ -657,10 +687,12 @@
             pltpu.VMEM((4, sibs, BLK), F32),
             pltpu.VMEM((sibs, BLK), F32),
             pltpu.VMEM((XH, Y, 2 * W, BLK), F32),
+            pltpu.VMEM((2 * ROWS, W, BLK), F32),
             pltpu.VMEM((ROWS, W, BLK), F32),
             pltpu.VMEM((ROWS, W, BLK), F32),
-            pltpu.VMEM((Y, W, BLK), F32),
-            pltpu.VMEM((ROWS * XH, 16, BLK), F32),
+            pltpu.VMEM((ROWS, W, BLK), F32),
+            pltpu.VMEM((WAVES, Y, W, BLK), F32),
+            pltpu.VMEM((WAVES * ROWS * XH, 16, BLK), F32),
             pltpu.VMEM((Z, 16, BLK), F32),
             pltpu.VMEM((Y, W, BLK), F32),
             pltpu.SMEM((ROWS,), jnp.int32),
@@ -680,16 +712,17 @@
             dma((8,)),
             dma((16,)),
             dma((16,)),
-            dma((ROWS,)),
-            dma((ROWS,)),
+            dma((2 * ROWS,)),
+            dma((2 * ROWS,)),
+            dma((2,)),
             dma((4, 8)),
             dma((4, 8)),
             dma((4, 8)),
             dma((4, 8)),
             dma((8,)),
             dma((2, 4)),
-            dma((ROWS * XH,)),
-            dma((ROWS * XH,)),
+            dma((WAVES * ROWS * XH,)),
+            dma((WAVES * ROWS * XH,)),
             dma((Z,)),
             dma((Z,)),
             dma((ROWS * XH,)),

time: 108 us -> 105 us (0.972)
  Pallas kernels: 106 us -> 103 us
    pallas_call x1, Pallas kernels: 106 us -> 103 us  [per_device(): pl.pallas_call(kernel, out_shape=tuple((pltpu.VMEM(out.shape, out.dtype)...]
where the time goes in v5:
time: 105 us
  Pallas kernels  103 us (98%)
  local copies, waits for them, and re-layouts  1.41 us (1%)
    pallas_call x1, Pallas kernels, per_device(): pl.pallas_call(kernel, out_shape=tuple((pltpu.VMEM(out.shape, out.dtype)...  103 us

profile of v5, /device:TPU:1, one launch (start us, length us, event | category | flops | bytes accessed | tf_op | source)
XLA Modules:
  0.0 105.1 jit_solution(14225165335631574933)
XLA Ops:
  0.6 103.0 %wave.1 = (f32[8,64,128]{2,1,0:T(8,128)S(1)}, f32[8,64,64]{2,1,0:T(8,128)S(1)}) custom-call(s32[8,32]{1,0:T(8,128)} %pattern.1, f32[8,64,256]{2,1,0:T(8,128)} %lower_hbm.1, f32[8,64,64]{2,1,0:T(8,128)} %diag_hbm.1, f32[8,2,128,512]{3,2,1,0:T(8,128)} %bitcast.1), custom_call_target="tpu_custom_call" | custom-call | tf_op jit(solution)/shard_map/wave/pallas_call | solution.py:668
  103.6 0.7 copy.8
  104.3 0.7 copy.9

commit v6 on v5

--- a/solution.py
+++ b/solution.py
@@ -306,7 +306,11 @@
     groups = (range(0, 2), range(2, 4), range(4, 6), range(6, 8))
 
     def kind(unit):
-        return unit // 2 % 2, unit // 4, unit % 2
+        return unit % 2, unit // 4, unit // 2 % 2
+
+    def first_row(g, item, dy, core):
+        index = order.index(dy)
+        return ((2 * item + index // 2) * 2 + g) * BLK + index % 2 * W + core * PART
 
     def start_y(g, item):
         y_copies[g, item, True].start()
@@ -328,7 +332,7 @@
         for dy in dys:
             core_copies[g, item, dy].wait_recv()
             for core in range(CORES):
-                start = (2 * item + g) * 256 + order.index(dy) * W + core * PART
+                start = first_row(g, item, dy, core)
                 high, low = halves(dense[g][spot(item, dy, core)])
                 dense_hi[start : start + PART, :] = high
                 dense_lo[start : start + PART, :] = low
@@ -438,9 +442,9 @@
         for dy in range(Y):
             squares = []
             for core in range(CORES):
-                start = item * 512 + order.index(dy) * W + core * PART
+                starts = [first_row(g, item, dy, core) for g in range(2)]
                 value = jnp.concatenate(
-                    [summed[start + g * 256 : start + g * 256 + PART, :] for g in range(2)], axis=0
+                    [summed[start : start + PART, :] for start in starts], axis=0
                 )
                 squares.append(dot_last(blocks[sibling(dy, core)], value, HIGHEST))
             update[item, (y + dy) % Y, :, :W] = jnp.where(k == 0, squares[0], squares[1])
@@ -475,38 +479,37 @@
     split_ancestor(1)
     split(0, 0, (0,))
     start_far(0, 0)
+    a_copies[2].start()
+    start_far(1, 0)
+    for d in range(3, Z):
+        a_copies[d].start()
+    split(0, 0, (1,))
+    split(1, 0, (0, 1))
+    multiply(0, 0, 1)
+    first_step(0)
     wave_copies[0].wait_recv()
     start_y(0, 1)
-    a_copies[2].start()
-    split(0, 0, (1, 3))
-    start_far(1, 0)
     wave_copies[1].wait_recv()
     start_y(1, 1)
-    for d in range(3, Z):
-        a_copies[d].start()
     end_far(0, 0)
-    split(1, 0, (0, 1, 3))
-    split(0, 0, (2,))
-    multiply(0, 0, 1)
-    first_step(0)
+    end_far(1, 0)
+    for g in range(2):
+        split(g, 0, (3, 2))
+    multiply(1, 0, 1)
+    first_step(1)
     start_far(0, 1)
-    end_far(1, 0)
     split_ancestor(2)
     multiply(0, 1, 2)
-    split(1, 0, (2,))
-    multiply(1, 0, 1)
-    first_step(1)
     next_step(0, 1)
     multiply(1, 1, 2)
     start_far(1, 1)
-    split(0, 1, (0, 1, 3))
     next_step(1, 1)
-    end_far(0, 1)
-    split(1, 1, (0, 1, 3))
-    split(0, 1, (2,))
+    for g in range(2):
+        split(g, 1, (0, 1))
     multiply(2, 0, 1)
     first_step(2)
     multiply(2, 1, 2)
+    end_far(0, 1)
     end_far(1, 1)
     block_copies = []
     for kept, into in enumerate((own_rows, pass_rows)):
@@ -522,7 +525,8 @@
             )
             copy.start()
             block_copies.append(copy)
-    split(1, 1, (2,))
+    for g in range(2):
+        split(g, 1, (3, 2))
     multiply(3, 0, 1)
     first_step(3)
     next_step(2, 1)

time: 105 us -> 104 us (level)
    pallas_call x1, Pallas kernels: 103 us -> 102 us  [per_device(): pl.pallas_call(kernel, out_shape=tuple((pltpu.VMEM(out.shape, out.dtype)...]
where the time goes in v6:
time: 104 us
  Pallas kernels  102 us (98%)
  local copies, waits for them, and re-layouts  1.41 us (1%)
    pallas_call x1, Pallas kernels, per_device(): pl.pallas_call(kernel, out_shape=tuple((pltpu.VMEM(out.shape, out.dtype)...  102 us

profile of v6, /device:TPU:1, one launch (start us, length us, event | category | flops | bytes accessed | tf_op | source)
XLA Modules:
  0.0 103.7 jit_solution(16273718472346417443)
XLA Ops:
  0.6 101.6 %wave.1 = (f32[8,64,128]{2,1,0:T(8,128)S(1)}, f32[8,64,64]{2,1,0:T(8,128)S(1)}) custom-call(s32[8,32]{1,0:T(8,128)} %pattern.1, f32[8,64,256]{2,1,0:T(8,128)} %lower_hbm.1, f32[8,64,64]{2,1,0:T(8,128)} %diag_hbm.1, f32[8,2,128,512]{3,2,1,0:T(8,128)} %bitcast.1), custom_call_target="tpu_custom_call" | custom-call | tf_op jit(solution)/shard_map/wave/pallas_call | solution.py:672
  102.3 0.7 copy.8
  103.0 0.7 copy.9

commit v7 on v6

--- a/solution.py
+++ b/solution.py
@@ -478,11 +478,11 @@
     split_ancestor(0)
     split_ancestor(1)
     split(0, 0, (0,))
+    a_copies[2].start()
     start_far(0, 0)
-    a_copies[2].start()
-    start_far(1, 0)
     for d in range(3, Z):
         a_copies[d].start()
+    start_far(1, 0)
     split(0, 0, (1,))
     split(1, 0, (0, 1))
     multiply(0, 0, 1)

time: 104 us -> 104 us (level)
  no operation moved by 1% of the time
where the time goes in v7:
time: 104 us
  Pallas kernels  102 us (98%)
  local copies, waits for them, and re-layouts  1.41 us (1%)
    pallas_call x1, Pallas kernels, per_device(): pl.pallas_call(kernel, out_shape=tuple((pltpu.VMEM(out.shape, out.dtype)...  102 us

profile of v7, /device:TPU:1, one launch (start us, length us, event | category | flops | bytes accessed | tf_op | source)
XLA Modules:
  0.0 103.6 jit_solution(7981287321989355841)
XLA Ops:
  0.6 101.6 %wave.1 = (f32[8,64,128]{2,1,0:T(8,128)S(1)}, f32[8,64,64]{2,1,0:T(8,128)S(1)}) custom-call(s32[8,32]{1,0:T(8,128)} %pattern.1, f32[8,64,256]{2,1,0:T(8,128)} %lower_hbm.1, f32[8,64,64]{2,1,0:T(8,128)} %diag_hbm.1, f32[8,2,128,512]{3,2,1,0:T(8,128)} %bitcast.1), custom_call_target="tpu_custom_call" | custom-call | tf_op jit(solution)/shard_map/wave/pallas_call | solution.py:672
  102.2 0.7 copy.8
  102.9 0.7 copy.9
